TPU v7x, 32 devices: a whole 2x2x4 slice. The times are simulated.
32 devices in a mesh: dp: 8 (over z, core), mp: 4 (over y, x).
Axes of the slice: x: 2, y: 2, z: 4, core: 2. Of those that a mesh axis runs over, the one named last changes fastest.
Arguments:
- activations: bfloat16 [4096, 8192], P('dp', 'mp')
- value_grad: bfloat16 [4096, 1024], P('dp'), may hold values from -6 to 6
- master: float32 [8192, 1024], P(('mp', 'dp')), may hold values from -6 to 6
- first_moment: float32 [8192, 1024], P(('mp', 'dp')), may hold values from -2 to 2
- second_moment: float32 [8192, 1024], P(('mp', 'dp')), may hold values from 0.05 to 1
- step_count: int32 [1], replicated, may hold values from 1 to 40
Outputs:
- new_master: float32 [8192, 1024], P(('mp', 'dp'))
- new_first: float32 [8192, 1024], P(('mp', 'dp'))
- new_second: float32 [8192, 1024], P(('mp', 'dp'))
- rollout_update: bfloat16 [8192, 1024], P(None, 'mp')
Inputs may be any that keep to these rules, and one draw needn't show every extreme that they name: `step_count`: the number of optimizer steps taken so far, this one included.
All inputs are finite; a program needn't handle non-finite values.
Results may differ from a plain program's by a relative error of at most 0.0004.
Values may be sent and summed in bfloat16 or wider, within the bound.
A program may use at most 64 MiB of HBM per device.

v0:
```python
import functools
import math

import jax
import jax.numpy as jnp
from jax import lax
from jax.experimental import pallas as pl
from jax.experimental.pallas import tpu as pltpu
from jax.sharding import PartitionSpec as P

F32 = jnp.float32
LEVELS = 32760.0
PIECES = (1, 1, 1, 4)
MESH = pl.DeviceIdType.MESH


def adam_terms(step):
    bias_first = 1.0 - jnp.exp(step * jnp.float32(math.log(0.9)))
    bias_second = 1.0 - jnp.exp(step * jnp.float32(math.log(0.95)))
    return 1.0 / bias_first, 1.0 / bias_second


def kernel(
    line,
    heads,
    chunks,
    clip_total,
    step_ref,
    act_ref,
    vg_ref,
    master_ref,
    first_ref,
    second_ref,
    new_master_ref,
    new_first_ref,
    new_second_ref,
    rollout_ref,
    act,
    vg,
    acc,
    q_out,
    s_out,
    q_in,
    s_in,
    norm_dp,
    norm_mp,
    w_in,
    m_in,
    v_in,
    w_out,
    m_out,
    v_out,
    update,
    in_sem,
    pair_send,
    pair_recv,
    load_sem,
    rs_send,
    rs_recv,
    norm_dp_send,
    norm_dp_recv,
    norm_mp_send,
    norm_mp_recv,
    store_sem,
    a2a_send,
    a2a_recv,
    up_send,
    down_send,
    chain_recv,
    mate_send,
    mate_recv,
):
    dpn = 2 * line
    dp = lax.axis_index("dp")
    mp = lax.axis_index("mp")
    z = dp // 2
    core = lax.rem(dp, 2)
    mate = dp + 1 - 2 * core
    tokens = act_ref.shape[0]
    rows = master_ref.shape[0]
    cols = master_ref.shape[1]
    tile = cols // chunks
    group = rows // 8
    head_cols = cols // heads

    barrier = pltpu.get_barrier_semaphore()
    for step in range(1, dpn):
        pl.semaphore_signal(
            barrier, inc=1, device_id={"dp": lax.rem(dp + step, dpn)}, device_id_type=MESH
        )
    for step in range(1, heads):
        pl.semaphore_signal(
            barrier, inc=1, device_id={"mp": lax.rem(mp + step, heads)}, device_id_type=MESH
        )

    lower = z < line // 2
    def owner(e):
        return jnp.where(lower, e, line - 1 - e)

    u = jnp.where(lower, z, line - 1 - z)

    def own_act(e):
        dest = owner(e)
        start = pl.multiple_of((dest * 2 + core) * rows, rows)
        return pltpu.make_async_copy(
            act_ref.at[:, pl.ds(start, rows)],
            act.at[dest, pl.ds(0, tokens)],
            in_sem.at[dest],
        )

    def own_vg(n):
        at = slice(n * tile, (n + 1) * tile)
        return pltpu.make_async_copy(
            vg_ref.at[:, at], vg.at[pl.ds(0, tokens), at], in_sem.at[line + n]
        )

    def pair_act(e):
        dest = owner(e)
        start = pl.multiple_of((dest * 2 + 1 - core) * rows, rows)
        return pltpu.make_async_remote_copy(
            src_ref=act_ref.at[:, pl.ds(start, rows)],
            dst_ref=act.at[dest, pl.ds(tokens, tokens)],
            send_sem=pair_send.at[dest],
            recv_sem=pair_recv.at[dest],
            device_id={"dp": mate},
            device_id_type=MESH,
        )

    def pair_vg(n):
        at = slice(n * tile, (n + 1) * tile)
        return pltpu.make_async_remote_copy(
            src_ref=vg_ref.at[:, at],
            dst_ref=vg.at[pl.ds(tokens, tokens), at],
            send_sem=pair_send.at[line + n],
            recv_sem=pair_recv.at[line + n],
            device_id={"dp": mate},
            device_id_type=MESH,
        )

    order = list(range(line - 1, -1, -1))
    own_act(order[0]).start()
    for n in range(chunks):
        own_vg(n).start()
    for e in order[1:]:
        own_act(e).start()
    loads = [
        pltpu.make_async_copy(src, dst, load_sem.at[i])
        for i, (src, dst) in enumerate(
            ((master_ref, w_in), (first_ref, m_in), (second_ref, v_in))
        )
    ]
    pl.semaphore_wait(barrier, dpn - 1 + heads - 1)
    pair_act(order[0]).start()
    for n in range(chunks):
        pair_vg(n).start()
    for e in order[1:]:
        pair_act(e).start()
    for copy in loads:
        copy.start()

    def multiply(dest, n):
        at = pl.ds(pl.multiple_of(n * tile, tile), tile)
        acc[dest, :, at] = lax.dot_general(
            act[dest], vg[:, at], (((0,), (0,)), ((), ())), preferred_element_type=F32
        )

    def hop(dest, way, chunk):
        to = (z + 1 - 2 * way) * 2 + core
        data = pltpu.make_async_remote_copy(
            src_ref=q_out.at[dest, chunk],
            dst_ref=q_in.at[way, dest, chunk],
            send_sem=rs_send.at[0, dest, chunk],
            recv_sem=rs_recv.at[0, way, dest, chunk],
            device_id={"dp": to},
            device_id_type=MESH,
        )
        scale = pltpu.make_async_remote_copy(
            src_ref=s_out.at[dest, chunk],
            dst_ref=s_in.at[way, dest, chunk],
            send_sem=rs_send.at[1, dest, chunk],
            recv_sem=rs_recv.at[1, way, dest, chunk],
            device_id={"dp": to},
            device_id_type=MESH,
        )
        return data, scale

    def take(dest, way, chunk):
        for copy in hop(dest, way, chunk):
            copy.wait_recv()
        lanes = pl.ds(pl.multiple_of(chunk * tile, tile), tile)
        top = s_in[way, dest, chunk] * (1.0 / LEVELS)
        for g in range(8):
            here = slice(g * group, (g + 1) * group)
            got = q_in[way, dest, chunk, here, :].astype(jnp.int32).astype(F32)
            acc[dest, here, lanes] += got * top

    def give(dest, way, chunk):
        lanes = pl.ds(pl.multiple_of(chunk * tile, tile), tile)
        peak = jnp.zeros((8, tile), F32)
        for g in range(rows // 8):
            peak = jnp.maximum(peak, jnp.abs(acc[dest, slice(g * 8, (g + 1) * 8), lanes]))
        top = jnp.maximum(jnp.max(peak, axis=0, keepdims=True), 1e-30)
        s_out[dest, chunk] = top
        ratio = LEVELS / top
        for g in range(8):
            here = slice(g * group, (g + 1) * group)
            total = acc[dest, here, lanes]
            q_out[dest, chunk, here, :] = (
                jnp.round(total * ratio).astype(jnp.int32).astype(jnp.int16)
            )
        for copy in hop(dest, way, chunk):
            copy.start()

    forward = jnp.where(lower, 0, 1)
    backward = 1 - forward

    def pass_forward(k):
        e = line - 1 - k
        dest = owner(e)

        @pl.when(u < e)
        def _():
            @pl.loop(0, chunks)
            def _(chunk):
                @pl.when(u > 0)
                def _():
                    take(dest, forward, chunk)

                give(dest, forward, chunk)

    def pass_backward(k):
        dest = owner(k)

        @pl.when(u > k)
        def _():
            @pl.loop(0, chunks)
            def _(chunk):
                take(dest, backward, chunk)
                give(dest, backward, chunk)

    far = owner(line - 1)
    own_act(line - 1).wait()
    pair_act(line - 1).wait_recv()
    for n in range(chunks):
        own_vg(n).wait()
        pair_vg(n).wait_recv()
        multiply(far, n)

        @pl.when(u == 0)
        def _():
            give(far, forward, n)

    for e in order[1:]:
        own_act(e).wait()
        pair_act(e).wait_recv()

        @pl.loop(0, chunks)
        def _(n):
            multiply(owner(e), n)

    @pl.when(u > 0)
    def _():
        pass_forward(0)

    for k in range(1, line - 1):
        pass_forward(k)
        if k - 1 < line // 2 - 1:
            pass_backward(k - 1)

    norm_dp[dp] = jnp.zeros(norm_dp.shape[1:], F32)

    @pl.loop(0, chunks)
    def _(chunk):
        take(z, backward, chunk)

        @pl.when(u > 0)
        def _():
            take(z, forward, chunk)

        lanes = pl.ds(pl.multiple_of(chunk * tile, tile), tile)
        square = jnp.zeros((8, tile), F32)
        for g in range(8):
            grad = acc[z, slice(g * group, (g + 1) * group), lanes]
            square += jnp.sum((grad * grad).reshape(group // 8, 8, tile), axis=0)
        for lane in range(0, tile, 128):
            norm_dp[dp] += square[:, lane : lane + 128]

    def norm_to_dp(step):
        return pltpu.make_async_remote_copy(
            src_ref=norm_dp.at[dp],
            dst_ref=norm_dp.at[dp],
            send_sem=norm_dp_send.at[step],
            recv_sem=norm_dp_recv.at[step],
            device_id={"dp": lax.rem(dp + step, dpn)},
            device_id_type=MESH,
        )

    def norm_to_mp(step):
        return pltpu.make_async_remote_copy(
            src_ref=norm_mp.at[mp],
            dst_ref=norm_mp.at[mp],
            send_sem=norm_mp_send.at[step],
            recv_sem=norm_mp_recv.at[step],
            device_id={"mp": lax.rem(mp + step, heads)},
            device_id_type=MESH,
        )

    for step in range(1, dpn):
        norm_to_dp(step).start()
    for copy in loads:
        copy.wait()
    for step in range(1, dpn):
        norm_to_dp(step).wait_recv()
    norm_mp[mp] = jnp.sum(norm_dp[...], axis=0)
    for step in range(1, heads):
        norm_to_mp(step).start()
    for step in range(1, heads):
        norm_to_mp(step).wait_recv()
    square_sum = jnp.sum(jnp.sum(norm_mp[...], axis=0), keepdims=True)
    factor = jnp.minimum(1.0, clip_total / (jnp.sqrt(square_sum) + 1e-06))
    step_count = jnp.full((1, 1), step_ref[0].astype(F32), F32)
    scale_first, scale_second = adam_terms(step_count)

    def block(head, origin):
        return rollout_ref.at[pl.ds(pl.multiple_of((head * dpn + origin) * rows, rows), rows)]

    mine = pltpu.make_async_copy(update.at[mp], block(mp, dp), store_sem.at[3])

    def to_head(step):
        head = lax.rem(mp + step, heads)
        return pltpu.make_async_remote_copy(
            src_ref=update.at[head],
            dst_ref=block(mp, dp),
            send_sem=a2a_send.at[step],
            recv_sem=a2a_recv.at[step],
            device_id={"mp": head},
            device_id_type=MESH,
        )

    def relay(source, head, at_z, send, recv, to):
        return pltpu.make_async_remote_copy(
            src_ref=source,
            dst_ref=block(head, at_z * 2 + core),
            send_sem=send.at[at_z, head],
            recv_sem=recv.at[at_z, head],
            device_id={"dp": to},
            device_id_type=MESH,
        )

    def send_up(source, head, at_z):
        return relay(source, head, at_z, up_send, chain_recv, dp + 2)

    def send_down(source, head, at_z):
        return relay(source, head, at_z, down_send, chain_recv, dp - 2)

    def send_mate(source, head, at_z):
        return relay(source, head, at_z, mate_send, mate_recv, mate)

    def spread(source, head):
        @pl.when(z < line - 1)
        def _():
            send_up(source, head, z).start()

        @pl.when(z > 0)
        def _():
            send_down(source, head, z).start()

        send_mate(source, head, z).start()

    slab = min(32, rows)
    for step in (*range(1, heads), 0):
        head = lax.rem(mp + step, heads)
        lanes = pl.ds(pl.multiple_of(head * head_cols, head_cols), head_cols)

        @pl.loop(0, rows // slab)
        def _(r):
            at = pl.ds(pl.multiple_of(r * slab, slab), slab)
            clipped = acc[z, at, lanes] * factor
            weight = w_in[at, lanes]
            first = 0.9 * m_in[at, lanes] + 0.1 * clipped
            second = 0.95 * v_in[at, lanes] + 0.05 * clipped * clipped
            m_out[at, lanes] = first
            v_out[at, lanes] = second
            direction = (first * scale_first) / (
                jnp.sqrt(second * scale_second) + 1e-08
            ) + 0.1 * weight
            w_out[at, lanes] = weight - 0.01 * direction
            update[head, at, :] = direction.astype(jnp.bfloat16)

        if step == 0:
            mine.start()
            spread(update.at[mp], mp)
        else:
            to_head(step).start()

    stores = [
        pltpu.make_async_copy(src, dst, store_sem.at[i])
        for i, (src, dst) in enumerate(
            ((w_out, new_master_ref), (m_out, new_first_ref), (v_out, new_second_ref))
        )
    ]
    for copy in stores:
        copy.start()

    for step in range(1, heads):
        head = lax.rem(mp + heads - step, heads)
        to_head(step).wait_recv()
        spread(block(head, dp), head)

    for far in range(1, line):
        for step in range(heads):
            head = lax.rem(mp + heads - step, heads)

            @pl.when(z - far >= 0)
            def _():
                at_z = z - far
                source = block(head, at_z * 2 + core)
                send_up(source, head, at_z).wait_recv()

                @pl.when(z < line - 1)
                def _():
                    send_up(source, head, at_z).start()

                send_mate(source, head, at_z).start()

            @pl.when(z + far < line)
            def _():
                at_z = z + far
                source = block(head, at_z * 2 + core)
                send_down(source, head, at_z).wait_recv()

                @pl.when(z > 0)
                def _():
                    send_down(source, head, at_z).start()

                send_mate(source, head, at_z).start()

    for at_z in range(line):
        for head in range(heads):
            source = block(head, at_z * 2 + core)
            send_mate(source, head, at_z).wait_recv()
            send_mate(source, head, at_z).wait_send()

            @pl.when((z < line - 1) & (z >= at_z))
            def _():
                send_up(source, head, at_z).wait_send()

            @pl.when((z > 0) & (z <= at_z))
            def _():
                send_down(source, head, at_z).wait_send()

    for step in range(1, heads):
        to_head(step).wait_send()
        norm_to_mp(step).wait_send()
    for step in range(1, dpn):
        norm_to_dp(step).wait_send()
    for dest in range(line):
        pair_act(dest).wait_send()

        @pl.when(z != dest)
        def _():
            @pl.loop(0, chunks)
            def _(chunk):
                for copy in hop(dest, 0, chunk):
                    copy.wait_send()

    for n in range(chunks):
        pair_vg(n).wait_send()
    mine.wait()
    for copy in stores:
        copy.wait()


def settle(*refs):
    count = (len(refs) - 1) // 2
    sem = refs[-1]
    copies = []
    for i in range(count):
        source, place = refs[i], refs[count + i]
        piece = source.shape[0] // PIECES[i]
        for j in range(PIECES[i]):
            at = pl.ds(j * piece, piece)
            copies.append(
                pltpu.make_async_copy(source.at[at], place.at[at], sem.at[len(copies)])
            )
    for copy in copies:
        copy.start()
    for copy in copies:
        copy.wait()


def one_kernel(line, heads, activations, value_grad, master, first_moment, second_moment, step_count):
    rows, cols = master.shape
    tokens = activations.shape[0]
    chunks = 4
    dpn = 2 * line
    clip_total = 0.5 * math.sqrt(rows * dpn * heads * cols)
    hbm = pl.BlockSpec(memory_space=pl.ANY)
    owned = jax.ShapeDtypeStruct((rows, cols), F32)
    wide = pltpu.VMEM((rows, cols), F32)
    dma = pltpu.SemaphoreType.DMA
    results = pl.pallas_call(
        functools.partial(kernel, line, heads, chunks, clip_total),
        out_shape=(
            owned,
            owned,
            owned,
            jax.ShapeDtypeStruct((rows * dpn * heads, cols // heads), jnp.bfloat16),
        ),
        in_specs=[pl.BlockSpec(memory_space=pltpu.SMEM)]
        + [hbm] * 5,
        out_specs=(hbm,) * 4,
        scratch_shapes=[
            pltpu.VMEM((line, 2 * tokens, rows), jnp.bfloat16),
            pltpu.VMEM((2 * tokens, cols), jnp.bfloat16),
            pltpu.VMEM((line, rows, cols), F32),
            pltpu.VMEM((line, chunks, rows, cols // chunks), jnp.int16),
            pltpu.VMEM((line, chunks, 1, cols // chunks), F32),
            pltpu.VMEM((2, line, chunks, rows, cols // chunks), jnp.int16),
            pltpu.VMEM((2, line, chunks, 1, cols // chunks), F32),
            pltpu.VMEM((dpn, 8, 128), F32),
            pltpu.VMEM((heads, 8, 128), F32),
            wide,
            wide,
            wide,
            wide,
            wide,
            wide,
            pltpu.VMEM((heads, rows, cols // heads), jnp.bfloat16),
            dma((line + chunks,)),
            dma((line + chunks,)),
            dma((line + chunks,)),
            dma((3,)),
            dma((2, line, chunks)),
            dma((2, 2, line, chunks)),
            dma((dpn,)),
            dma((dpn,)),
            dma((heads,)),
            dma((heads,)),
            dma((4,)),
            dma((heads,)),
            dma((heads,)),
            dma((line, heads)),
            dma((line, heads)),
            dma((line, heads)),
            dma((line, heads)),
            dma((line, heads)),
        ],
        compiler_params=pltpu.CompilerParams(
            collective_id=0, has_side_effects=True, vmem_limit_bytes=28 * 1024 * 1024
        ),
    )(
        step_count,
        *(
            pltpu.with_memory_space_constraint(x, pltpu.HBM)
            for x in (activations, value_grad, master, first_moment, second_moment)
        ),
    )
    shapes = tuple(jax.ShapeDtypeStruct(x.shape, x.dtype) for x in results)
    return pl.pallas_call(
        settle,
        out_shape=shapes,
        in_specs=[hbm] * 4,
        out_specs=(hbm,) * 4,
        scratch_shapes=[dma((sum(PIECES),))],
        compiler_params=pltpu.CompilerParams(vmem_limit_bytes=4 * 1024 * 1024),
    )(*(pltpu.with_memory_space_constraint(x, pltpu.VMEM) for x in results))


def plain(activations, value_grad, master, first_moment, second_moment, step_count):
    own_rows, cols = master.shape
    grad = lax.psum_scatter(
        lax.dot_general(
            activations, value_grad, (((0,), (0,)), ((), ())), preferred_element_type=F32
        ),
        "dp",
        scatter_dimension=0,
        tiled=True,
    )
    square_sum = lax.psum(jnp.sum(grad * grad), ("dp", "mp"))
    head_count = lax.axis_size("mp")
    clip_total = 0.5 * math.sqrt(own_rows * lax.axis_size("dp") * head_count * cols)
    factor = jnp.minimum(jnp.float32(1.0), clip_total / (jnp.sqrt(square_sum) + 1e-06))
    clipped = factor * grad
    new_first = 0.9 * first_moment + 0.1 * clipped
    new_second = 0.95 * second_moment + 0.05 * clipped * clipped
    scale_first, scale_second = adam_terms(step_count[0].astype(F32))
    direction = new_first * scale_first / (jnp.sqrt(new_second * scale_second) + 1e-08) + 0.1 * master
    new_master = master - 0.01 * direction
    update = direction.astype(jnp.bfloat16)
    received = lax.all_to_all(update, "mp", split_axis=1, concat_axis=0, tiled=True)
    stacked = received.reshape(head_count, own_rows, received.shape[1])
    gathered = lax.all_gather(stacked, "dp", axis=1, tiled=True)
    return (new_master, new_first, new_second, gathered.reshape(-1, gathered.shape[2]))


def solution(mesh):
    dpn, heads = mesh.shape["dp"], mesh.shape["mp"]

    def on_device(*args):
        rows, cols = args[2].shape
        if dpn % 4 == 0 and dpn <= 16 and rows % 128 == 0 and (cols // heads) % 128 == 0:
            return one_kernel(dpn // 2, heads, *args)
        return plain(*args)

    in_specs = (
        P("dp", "mp"),
        P("dp", None),
        P(("mp", "dp"), None),
        P(("mp", "dp"), None),
        P(("mp", "dp"), None),
        P(),
    )
    out_specs = (P(("mp", "dp"), None), P(("mp", "dp"), None), P(("mp", "dp"), None), P(None, "mp"))
    return jax.shard_map(
        on_device, mesh=mesh, in_specs=in_specs, out_specs=out_specs, check_vma=False
    )
```

profile of v0, /device:TPU:0, one launch (start us, length us, event | category | flops | bytes accessed | tf_op | source)
XLA Modules:
  0.0 98.2 jit_solution(4206466143663714833)
XLA Ops:
  1.3 93.8 %shard_map.93 = (f32[256,1024]{1,0:T(8,128)S(1)}, f32[256,1024]{1,0:T(8,128)S(1)}, f32[256,1024]{1,0:T(8,128)S(1)}, bf16[8192,256]{1,0:T(8,128)(2,1)S(1)}) custom-call(s32[1]{0:T(128)S(6)} %copy.10.step_ref, bf16[512,2048]{1,0:T(8,128)(2,1)} %act_ref.1, bf16[512,1024]{1,0:T(8,128)(2,1)} %vg_ref.1, f32[256,1024]{1,0:T(8,128)} %master_ref.1, ...), custom_call_target="tpu_custom_call" | custom-call | tf_op jit(solution)/shard_map/pallas_call | solution.py:502
  95.1 3.0 %shard_map.94 = (f32[256,1024]{1,0:T(8,128)}, f32[256,1024]{1,0:T(8,128)}, f32[256,1024]{1,0:T(8,128)}, bf16[8192,256]{1,0:T(8,128)(2,1)}) custom-call(f32[256,1024]{1,0:T(8,128)S(1)} %get-tuple-element.8.refs_0_, f32[256,1024]{1,0:T(8,128)S(1)} %get-tuple-element.9.refs_1_, f32[256,1024]{1,0:T(8,128)S(1)} %get-tuple-element.10.refs_2_, ...), custom_call_target="tpu_custom_call" | custom-call | tf_op jit(solution)/shard_map/pallas_call | solution.py:560
where the time goes:
time: 98.3 us; the launch traced here: 98.2 us
  Pallas kernels  96.9 us (99%)
  between operations  1.29 us (1%)
    pallas_call x1, Pallas kernels, one_kernel(): pl.pallas_call(functools.partial(kernel, line, heads, chunks, clip_total)...  93.8 us
    pallas_call x1, Pallas kernels, one_kernel(): pl.pallas_call(settle, out_shape=shapes, in_specs=[hbm] * 4, out_specs=(h...  3.05 us

commit v1 on v0

v1 whole, which is shorter than its diff:
```python
import functools
import math

import jax
import jax.numpy as jnp
from jax import lax
from jax.experimental import pallas as pl
from jax.experimental.pallas import tpu as pltpu
from jax.sharding import PartitionSpec as P

F32 = jnp.float32
LEVELS = 32760.0
PIECES = (1, 1, 1, 4)
RES = 2
LAG = 2
MESH = pl.DeviceIdType.MESH


def adam_terms(step):
    bias_first = 1.0 - jnp.exp(step * jnp.float32(math.log(0.9)))
    bias_second = 1.0 - jnp.exp(step * jnp.float32(math.log(0.95)))
    return 1.0 / bias_first, 1.0 / bias_second


def kernel(
    line,
    heads,
    clip_total,
    step_ref,
    act_ref,
    vg_ref,
    master_ref,
    first_ref,
    second_ref,
    new_master_ref,
    new_first_ref,
    new_second_ref,
    rollout_ref,
    act,
    vg,
    acc,
    q_out,
    s_out,
    q_in,
    s_in,
    squares,
    norms,
    w_in,
    m_in,
    v_in,
    w_out,
    m_out,
    v_out,
    update,
    in_sem,
    pair_send,
    pair_recv,
    load_sem,
    rs_send,
    rs_recv,
    meet,
    norm_send,
    norm_recv,
    store_sem,
    a2a_send,
    a2a_recv,
    up_send,
    down_send,
    chain_recv,
    mate_send,
    mate_recv,
):
    dpn = 2 * line
    dp = lax.axis_index("dp")
    mp = lax.axis_index("mp")
    z = dp // 2
    core = lax.rem(dp, 2)
    mate = dp + 1 - 2 * core
    tokens = act_ref.shape[0]
    rows = master_ref.shape[0]
    cols = master_ref.shape[1]
    head_cols = cols // heads
    tile = head_cols // 2
    chunks = 2 * heads
    half = rows // 2

    lower = z < line // 2
    at_end = (z == 0) | (z == line - 1)
    end = jnp.where(lower, 0, line - 1)
    mid = jnp.where(lower, 1, line - 2)
    far_mid = line - 1 - mid
    far_end = line - 1 - end
    toward = jnp.where(lower, 2, -2)
    ahead = dp + toward
    behind = jnp.where(at_end, dp, dp - toward)

    def peer(slot):
        return lax.rem(mp // 2 + slot // 2, heads // 2) * 2 + lax.rem(mp + slot % 2, 2)

    def source(slot):
        y = lax.rem(mp // 2 + heads // 2 - slot // 2, heads // 2)
        return y * 2 + lax.rem(mp + slot % 2, 2)

    barrier = pltpu.get_barrier_semaphore()
    pl.semaphore_signal(barrier, inc=1, device_id={"dp": mate}, device_id_type=MESH)
    pl.semaphore_signal(barrier, inc=1, device_id={"dp": ahead}, device_id_type=MESH)

    @pl.when(jnp.logical_not(at_end))
    def _():
        pl.semaphore_signal(barrier, inc=1, device_id={"dp": behind}, device_id_type=MESH)

    for slot in (1, 2):
        pl.semaphore_signal(barrier, inc=1, device_id={"mp": peer(slot)}, device_id_type=MESH)

    def own_act(dest):
        start = pl.multiple_of((dest * 2 + core) * rows, rows)
        return pltpu.make_async_copy(
            act_ref.at[:, pl.ds(start, rows)],
            act.at[dest, pl.ds(0, tokens)],
            in_sem.at[dest],
        )

    def head_lanes(slot):
        return pl.ds(pl.multiple_of(peer(slot) * head_cols, head_cols), head_cols)

    def chunk_lanes(k):
        at = peer(k // 2) * 2 + k % 2
        return pl.ds(pl.multiple_of(at * tile, tile), tile)

    def own_vg(slot):
        at = head_lanes(slot)
        return pltpu.make_async_copy(
            vg_ref.at[:, at], vg.at[pl.ds(0, tokens), at], in_sem.at[line + slot]
        )

    def pair_act(dest):
        start = pl.multiple_of((dest * 2 + 1 - core) * rows, rows)
        return pltpu.make_async_remote_copy(
            src_ref=act_ref.at[:, pl.ds(start, rows)],
            dst_ref=act.at[dest, pl.ds(tokens, tokens)],
            send_sem=pair_send.at[dest],
            recv_sem=pair_recv.at[dest],
            device_id={"dp": mate},
            device_id_type=MESH,
        )

    def pair_vg(slot):
        at = head_lanes(slot)
        return pltpu.make_async_remote_copy(
            src_ref=vg_ref.at[:, at],
            dst_ref=vg.at[pl.ds(tokens, tokens), at],
            send_sem=pair_send.at[line + slot],
            recv_sem=pair_recv.at[line + slot],
            device_id={"dp": mate},
            device_id_type=MESH,
        )

    order = [
        far_end,
        jnp.where(at_end, far_mid, end),
        jnp.where(at_end, mid, far_mid),
        jnp.where(at_end, end, mid),
    ]
    own_act(order[0]).start()
    for slot in range(heads):
        own_vg(slot).start()
    for dest in order[1:]:
        own_act(dest).start()
    loads = [
        pltpu.make_async_copy(src, dst, load_sem.at[i])
        for i, (src, dst) in enumerate(
            ((master_ref, w_in), (first_ref, m_in), (second_ref, v_in))
        )
    ]
    with jax.named_scope("bar"):
        pl.semaphore_wait(barrier, jnp.where(at_end, 4, 5))
    pair_act(order[0]).start()
    for slot in range(heads):
        pair_vg(slot).start()
    for dest in order[1:]:
        pair_act(dest).start()
    for copy in loads:
        copy.start()

    def ready(dest):
        own_act(dest).wait()
        pair_act(dest).wait_recv()

    def multiply(dest, slot):
        at = head_lanes(slot)
        acc[dest, :, at] = lax.dot_general(
            act[dest], vg[:, at], (((0,), (0,)), ((), ())), preferred_element_type=F32
        )

    def hop(dest, k, way, to):
        data = pltpu.make_async_remote_copy(
            src_ref=q_out.at[dest, k],
            dst_ref=q_in.at[way, dest, k],
            send_sem=rs_send.at[0, dest, k],
            recv_sem=rs_recv.at[0, way, dest, k],
            device_id={"dp": to},
            device_id_type=MESH,
        )
        scale = pltpu.make_async_remote_copy(
            src_ref=s_out.at[dest, k],
            dst_ref=s_in.at[way, dest, k],
            send_sem=rs_send.at[1, dest, k],
            recv_sem=rs_recv.at[1, way, dest, k],
            device_id={"dp": to},
            device_id_type=MESH,
        )
        return data, scale

    def take(dest, k, way):
        for copy in hop(dest, k, way, ahead):
            copy.wait_recv()
        top = s_in[way, dest, k] * (1.0 / LEVELS)
        got = q_in[way, dest, k].astype(jnp.int32).astype(F32)
        return acc[dest, :, chunk_lanes(k)] + got * top

    def give(total, dest, k, way, to):
        top = jnp.maximum(jnp.max(jnp.abs(total), axis=0, keepdims=True), 1e-30)
        s_out[dest, k] = top
        q_out[dest, k] = jnp.round(total * (LEVELS / top)).astype(jnp.int32).astype(jnp.int16)
        for copy in hop(dest, k, way, to):
            copy.start()

    def add_squares(total):
        squares[...] += jnp.sum((total * total).reshape(rows // 8, 8, tile), axis=0)

    def place(i, first, second):
        dest = jnp.where(i < chunks, first, second)
        return dest, jnp.where(i < chunks, i, lax.rem(i + RES, chunks))

    squares[...] = jnp.zeros(squares.shape, F32)

    with jax.named_scope("w0"):
        ready(order[0])

    def hello(stage):
        slot = stage + 1
        pl.semaphore_signal(
            meet.at[stage], inc=1, device_id={"mp": peer(slot)}, device_id_type=MESH
        )

    def heard(stage):
        pl.semaphore_wait(meet.at[stage], 1)

    @pl.when(at_end)
    def _():
        def send(dest, k):
            give(acc[dest, :, chunk_lanes(k)], dest, k, 0, ahead)

        for slot in range(heads):
            own_vg(slot).wait()
            pair_vg(slot).wait_recv()
            with jax.named_scope(f"Em{slot}"):
                multiply(far_end, slot)
            with jax.named_scope(f"Eg{slot}"):
                send(far_end, 2 * slot)
                send(far_end, 2 * slot + 1)

        with jax.named_scope("Erest"):
            ready(far_mid)

            @pl.loop(0, heads)
            def _(step):
                slot = lax.rem(step + RES // 2, heads)
                multiply(far_mid, slot)
                send(far_mid, 2 * slot)
                send(far_mid, 2 * slot + 1)

            ready(mid)

            @pl.loop(0, heads)
            def _(slot):
                multiply(mid, slot)
                send(mid, 2 * slot)
                send(mid, 2 * slot + 1)

            ready(end)

            @pl.loop(0, heads)
            def _(slot):
                multiply(end, slot)

        @pl.loop(0, 2 * chunks - RES)
        def _(j):
            with jax.named_scope("Et"):
                dest, k = place(j, end, mid)
                total = take(dest, k, 1)
                add_squares(total)

                @pl.when(j < chunks)
                def _():
                    acc[dest, :, chunk_lanes(k)] = total

                @pl.when(j == 1)
                def _():
                    hello(0)

                @pl.when(j == chunks // 2)
                def _():
                    heard(0)
                    hello(1)

        heard(1)

    @pl.when(jnp.logical_not(at_end))
    def _():
        for slot in range(heads):
            own_vg(slot).wait()
            pair_vg(slot).wait_recv()
            multiply(far_end, slot)
        ready(end)

        @pl.loop(0, heads)
        def _(slot):
            multiply(end, slot)

        ready(far_mid)
        ready(mid)

        def onward(j):
            dest, k = place(j, end, mid)
            total = take(dest, k, 1)

            @pl.when(j < 2 * chunks - RES)
            def _():
                give(total, dest, k, 1, behind)

            @pl.when(j >= chunks)
            def _():
                acc[dest, :, chunk_lanes(k)] = total

        @pl.loop(0, 2 * chunks)
        def _(i):
            with jax.named_scope("Mn"):
                dest, k = place(i, far_end, far_mid)
                give(take(dest, k, 0), dest, k, 1, ahead)

            @pl.when(i < chunks)
            def _():
                multiply(jnp.where(i < heads, far_mid, mid), lax.rem(i, heads))

            @pl.when(i >= LAG)
            def _():
                with jax.named_scope("Mf"):
                    onward(i - LAG)

            @pl.when(i == LAG + 1)
            def _():
                hello(0)

            @pl.when(i == LAG + chunks // 2)
            def _():
                heard(0)
                hello(1)

        @pl.loop(2 * chunks - LAG, 2 * chunks - RES)
        def _(j):
            with jax.named_scope("Mf"):
                onward(j)

        for k in range(RES):
            with jax.named_scope("Mr"):
                onward(2 * chunks - RES + k)
                total = take(mid, k, 0)
                acc[mid, :, chunk_lanes(k)] = total
                add_squares(total)

        heard(1)

    me = dp * heads + mp
    norms[me] = jnp.sum(squares[...], axis=0, keepdims=True)

    def norm_to(step, slot):
        at = step * heads + slot
        return pltpu.make_async_remote_copy(
            src_ref=norms.at[me],
            dst_ref=norms.at[me],
            send_sem=norm_send.at[at],
            recv_sem=norm_recv.at[at],
            device_id={"dp": lax.rem(dp + step, dpn), "mp": lax.rem(mp + slot, heads)},
            device_id_type=MESH,
        )

    others = [(step, slot) for step in range(dpn) for slot in range(heads) if step + slot]
    with jax.named_scope("ns"):
        for step, slot in others:
            norm_to(step, slot).start()
    for copy in loads:
        copy.wait()
    with jax.named_scope("nw"):
        for step, slot in others:
            norm_to(step, slot).wait_recv()
    square_sum = jnp.sum(jnp.sum(norms[...], axis=0), keepdims=True)
    factor = jnp.minimum(1.0, clip_total / (jnp.sqrt(square_sum) + 1e-06))
    step_count = jnp.full((1, 1), step_ref[0].astype(F32), F32)
    scale_first, scale_second = adam_terms(step_count)

    def block(owner, origin, part):
        start = (owner * dpn + origin) * rows + part * half
        return rollout_ref.at[pl.ds(pl.multiple_of(start, half), half)]

    def piece(head, part):
        return update.at[head, pl.ds(part * half, half)]

    def mine(part):
        return pltpu.make_async_copy(
            piece(mp, part), block(mp, dp, part), store_sem.at[3 + part]
        )

    def to_head(slot, part):
        return pltpu.make_async_remote_copy(
            src_ref=piece(peer(slot), part),
            dst_ref=block(mp, dp, part),
            send_sem=a2a_send.at[slot, part],
            recv_sem=a2a_recv.at[slot, part],
            device_id={"mp": peer(slot)},
            device_id_type=MESH,
        )

    def relay(ref, owner, at_z, part, send, recv, to):
        return pltpu.make_async_remote_copy(
            src_ref=ref,
            dst_ref=block(owner, at_z * 2 + core, part),
            send_sem=send.at[at_z, owner, part],
            recv_sem=recv.at[at_z, owner, part],
            device_id={"dp": to},
            device_id_type=MESH,
        )

    def send_up(ref, owner, at_z, part):
        return relay(ref, owner, at_z, part, up_send, chain_recv, dp + 2)

    def send_down(ref, owner, at_z, part):
        return relay(ref, owner, at_z, part, down_send, chain_recv, dp - 2)

    def send_mate(ref, owner, at_z, part):
        return relay(ref, owner, at_z, part, mate_send, mate_recv, mate)

    def spread(ref, owner, part):
        @pl.when(z < line - 1)
        def _():
            send_up(ref, owner, z, part).start()

        @pl.when(z > 0)
        def _():
            send_down(ref, owner, z, part).start()

        send_mate(ref, owner, z, part).start()

    slab = min(32, half)

    def step_rows(slot, part):
        lanes = head_lanes(slot)

        @pl.loop(0, half // slab)
        def _(r):
            at = pl.ds(pl.multiple_of(part * half + r * slab, slab), slab)
            clipped = acc[z, at, lanes] * factor
            weight = w_in[at, lanes]
            first = 0.9 * m_in[at, lanes] + 0.1 * clipped
            second = 0.95 * v_in[at, lanes] + 0.05 * clipped * clipped
            m_out[at, lanes] = first
            v_out[at, lanes] = second
            direction = (first * scale_first) / (
                jnp.sqrt(second * scale_second) + 1e-08
            ) + 0.1 * weight
            w_out[at, lanes] = weight - 0.01 * direction
            update[peer(slot), at, :] = direction.astype(jnp.bfloat16)

    def late(slot):
        @pl.when(jnp.logical_not(at_end))
        def _():
            for k in (2 * slot, 2 * slot + 1):
                acc[mid, :, chunk_lanes(k)] = take(mid, k, 0)

    work = [(0, 0), (1, 0), (2, 0), (0, 1), (1, 1), (2, 1), (3, 0), (3, 1)]
    for slot, part in work:
        with jax.named_scope(f"up{slot}{part}"):
            if part == 0 and 2 * slot >= RES:
                late(slot)
            step_rows(slot, part)
            if slot == 0:
                mine(part).start()
                spread(piece(mp, part), mp, part)
            else:
                to_head(slot, part).start()

    stores = [
        pltpu.make_async_copy(src, dst, store_sem.at[i])
        for i, (src, dst) in enumerate(
            ((w_out, new_master_ref), (m_out, new_first_ref), (v_out, new_second_ref))
        )
    ]
    for copy in stores:
        copy.start()

    for slot, part in work:
        if slot:
            with jax.named_scope(f"aa{slot}{part}"):
                to_head(slot, part).wait_recv()
                spread(block(source(slot), dp, part), source(slot), part)

    arrivals = [(0, 0), (0, 1)] + [w for w in work if w[0]]
    for far in range(1, line):
        with jax.named_scope(f"far{far}"):
            for slot, part in arrivals:
                owner = source(slot)

                @pl.when(z - far >= 0)
                def _():
                    at_z = z - far
                    ref = block(owner, at_z * 2 + core, part)
                    send_up(ref, owner, at_z, part).wait_recv()

                    @pl.when(z < line - 1)
                    def _():
                        send_up(ref, owner, at_z, part).start()

                    send_mate(ref, owner, at_z, part).start()

                @pl.when(z + far < line)
                def _():
                    at_z = z + far
                    ref = block(owner, at_z * 2 + core, part)
                    send_down(ref, owner, at_z, part).wait_recv()

                    @pl.when(z > 0)
                    def _():
                        send_down(ref, owner, at_z, part).start()

                    send_mate(ref, owner, at_z, part).start()

    with jax.named_scope("tail"):
        for at_z in range(line):
            for owner in range(heads):
                for part in range(2):
                    ref = block(owner, at_z * 2 + core, part)
                    send_mate(ref, owner, at_z, part).wait_recv()
                    send_mate(ref, owner, at_z, part).wait_send()

                    @pl.when((z < line - 1) & (z >= at_z))
                    def _():
                        send_up(ref, owner, at_z, part).wait_send()

                    @pl.when((z > 0) & (z <= at_z))
                    def _():
                        send_down(ref, owner, at_z, part).wait_send()

        for slot in range(1, heads):
            for part in range(2):
                to_head(slot, part).wait_send()
        for step, slot in others:
            norm_to(step, slot).wait_send()
        for dest in range(line):
            pair_act(dest).wait_send()
        for slot in range(heads):
            pair_vg(slot).wait_send()

        def sent(dest, k):
            for copy in hop(dest, k, 0, ahead):
                copy.wait_send()

        @pl.loop(0, chunks)
        def _(k):
            sent(far_end, k)
            sent(far_mid, k)
            sent(jnp.where(at_end, mid, end), k)

            @pl.when(jnp.logical_not(at_end) & (k >= RES))
            def _():
                sent(mid, k)

        for part in range(2):
            mine(part).wait()
        for copy in stores:
            copy.wait()


def settle(*refs):
    count = (len(refs) - 1) // 2
    sem = refs[-1]
    copies = []
    for i in range(count):
        source, place = refs[i], refs[count + i]
        piece = source.shape[0] // PIECES[i]
        for j in range(PIECES[i]):
            at = pl.ds(j * piece, piece)
            copies.append(
                pltpu.make_async_copy(source.at[at], place.at[at], sem.at[len(copies)])
            )
    for copy in copies:
        copy.start()
    for copy in copies:
        copy.wait()


def one_kernel(line, heads, activations, value_grad, master, first_moment, second_moment, step_count):
    rows, cols = master.shape
    tokens = activations.shape[0]
    tile = cols // heads // 2
    chunks = 2 * heads
    dpn = 2 * line
    clip_total = 0.5 * math.sqrt(rows * dpn * heads * cols)
    hbm = pl.BlockSpec(memory_space=pl.ANY)
    owned = jax.ShapeDtypeStruct((rows, cols), F32)
    wide = pltpu.VMEM((rows, cols), F32)
    dma = pltpu.SemaphoreType.DMA
    results = pl.pallas_call(
        functools.partial(kernel, line, heads, clip_total),
        out_shape=(
            owned,
            owned,
            owned,
            jax.ShapeDtypeStruct((rows * dpn * heads, cols // heads), jnp.bfloat16),
        ),
        in_specs=[pl.BlockSpec(memory_space=pltpu.SMEM)]
        + [hbm] * 5,
        out_specs=(hbm,) * 4,
        scratch_shapes=[
            pltpu.VMEM((line, 2 * tokens, rows), jnp.bfloat16),
            pltpu.VMEM((2 * tokens, cols), jnp.bfloat16),
            pltpu.VMEM((line, rows, cols), F32),
            pltpu.VMEM((line, chunks, rows, tile), jnp.int16),
            pltpu.VMEM((line, chunks, 1, tile), F32),
            pltpu.VMEM((2, line, chunks, rows, tile), jnp.int16),
            pltpu.VMEM((2, line, chunks, 1, tile), F32),
            pltpu.VMEM((8, tile), F32),
            pltpu.VMEM((dpn * heads, 1, tile), F32),
            wide,
            wide,
            wide,
            wide,
            wide,
            wide,
            pltpu.VMEM((heads, rows, cols // heads), jnp.bfloat16),
            dma((line + heads,)),
            dma((line + heads,)),
            dma((line + heads,)),
            dma((3,)),
            dma((2, line, chunks)),
            dma((2, 2, line, chunks)),
            pltpu.SemaphoreType.REGULAR((2,)),
            dma((dpn * heads,)),
            dma((dpn * heads,)),
            dma((5,)),
            dma((heads, 2)),
            dma((heads, 2)),
            dma((line, heads, 2)),
            dma((line, heads, 2)),
            dma((line, heads, 2)),
            dma((line, heads, 2)),
            dma((line, heads, 2)),
        ],
        compiler_params=pltpu.CompilerParams(
            collective_id=0, has_side_effects=True, vmem_limit_bytes=28 * 1024 * 1024
        ),
    )(
        step_count,
        *(
            pltpu.with_memory_space_constraint(x, pltpu.HBM)
            for x in (activations, value_grad, master, first_moment, second_moment)
        ),
    )
    shapes = tuple(jax.ShapeDtypeStruct(x.shape, x.dtype) for x in results)
    return pl.pallas_call(
        settle,
        out_shape=shapes,
        in_specs=[hbm] * 4,
        out_specs=(hbm,) * 4,
        scratch_shapes=[dma((sum(PIECES),))],
        compiler_params=pltpu.CompilerParams(vmem_limit_bytes=4 * 1024 * 1024),
    )(*(pltpu.with_memory_space_constraint(x, pltpu.VMEM) for x in results))


def plain(activations, value_grad, master, first_moment, second_moment, step_count):
    own_rows, cols = master.shape
    grad = lax.psum_scatter(
        lax.dot_general(
            activations, value_grad, (((0,), (0,)), ((), ())), preferred_element_type=F32
        ),
        "dp",
        scatter_dimension=0,
        tiled=True,
    )
    square_sum = lax.psum(jnp.sum(grad * grad), ("dp", "mp"))
    head_count = lax.axis_size("mp")
    clip_total = 0.5 * math.sqrt(own_rows * lax.axis_size("dp") * head_count * cols)
    factor = jnp.minimum(jnp.float32(1.0), clip_total / (jnp.sqrt(square_sum) + 1e-06))
    clipped = factor * grad
    new_first = 0.9 * first_moment + 0.1 * clipped
    new_second = 0.95 * second_moment + 0.05 * clipped * clipped
    scale_first, scale_second = adam_terms(step_count[0].astype(F32))
    direction = new_first * scale_first / (jnp.sqrt(new_second * scale_second) + 1e-08) + 0.1 * master
    new_master = master - 0.01 * direction
    update = direction.astype(jnp.bfloat16)
    received = lax.all_to_all(update, "mp", split_axis=1, concat_axis=0, tiled=True)
    stacked = received.reshape(head_count, own_rows, received.shape[1])
    gathered = lax.all_gather(stacked, "dp", axis=1, tiled=True)
    return (new_master, new_first, new_second, gathered.reshape(-1, gathered.shape[2]))


def solution(mesh):
    dpn, heads = mesh.shape["dp"], mesh.shape["mp"]

    def on_device(*args):
        rows, cols = args[2].shape
        if dpn == 8 and heads == 4 and rows % 64 == 0 and (cols // heads) % 256 == 0:
            return one_kernel(dpn // 2, heads, *args)
        return plain(*args)

    in_specs = (
        P("dp", "mp"),
        P("dp", None),
        P(("mp", "dp"), None),
        P(("mp", "dp"), None),
        P(("mp", "dp"), None),
        P(),
    )
    out_specs = (P(("mp", "dp"), None), P(("mp", "dp"), None), P(("mp", "dp"), None), P(None, "mp"))
    return jax.shard_map(
        on_device, mesh=mesh, in_specs=in_specs, out_specs=out_specs, check_vma=False
    )
```

time: 98.3 us -> 90.8 us (0.924)
  Pallas kernels: 96.9 us -> 89.3 us
    pallas_call x1, Pallas kernels: 93.8 us -> 86.3 us  [one_kernel(): pl.pallas_call(functools.partial(kernel, line, heads, clip_total), out_sh...]
where the time goes in v1:
time: 90.8 us; the launch traced here: 90.6 us
  Pallas kernels  89.3 us (98%)
  between operations  1.29 us (1%)
    pallas_call x1, Pallas kernels, one_kernel(): pl.pallas_call(functools.partial(kernel, line, heads, clip_total), out_sh...  86.3 us
    pallas_call x1, Pallas kernels, one_kernel(): pl.pallas_call(settle, out_shape=shapes, in_specs=[hbm] * 4, out_specs=(h...  3.05 us

profile of v1, /device:TPU:0, one launch (start us, length us, event | category | flops | bytes accessed | tf_op | source)
XLA Modules:
  0.0 90.6 jit_solution(5831105637067059118)
XLA Ops:
  1.3 86.3 %shard_map.93 = (f32[256,1024]{1,0:T(8,128)S(1)}, f32[256,1024]{1,0:T(8,128)S(1)}, f32[256,1024]{1,0:T(8,128)S(1)}, bf16[8192,256]{1,0:T(8,128)(2,1)S(1)}) custom-call(s32[1]{0:T(128)S(6)} %copy.10.step_ref, bf16[512,2048]{1,0:T(8,128)(2,1)} %act_ref.1, bf16[512,1024]{1,0:T(8,128)(2,1)} %vg_ref.1, f32[256,1024]{1,0:T(8,128)} %master_ref.1, ...), custom_call_target="tpu_custom_call" | custom-call | tf_op jit(solution)/shard_map/pallas_call | solution.py:612
  87.6 3.0 %shard_map.94 = (f32[256,1024]{1,0:T(8,128)}, f32[256,1024]{1,0:T(8,128)}, f32[256,1024]{1,0:T(8,128)}, bf16[8192,256]{1,0:T(8,128)(2,1)}) custom-call(f32[256,1024]{1,0:T(8,128)S(1)} %get-tuple-element.8.refs_0_, f32[256,1024]{1,0:T(8,128)S(1)} %get-tuple-element.9.refs_1_, f32[256,1024]{1,0:T(8,128)S(1)} %get-tuple-element.10.refs_2_, ...), custom_call_target="tpu_custom_call" | custom-call | tf_op jit(solution)/shard_map/pallas_call | solution.py:669

commit v2 on v1

v2 whole, which is shorter than its diff:
```python
import functools
import math

import jax
import jax.numpy as jnp
from jax import lax
from jax.experimental import pallas as pl
from jax.experimental.pallas import tpu as pltpu
from jax.sharding import PartitionSpec as P

F32 = jnp.float32
LEVELS = 32760.0
PIECES = (1, 1, 1, 4)
RES = 4
LAG = 4
EARLY = 4
MESH = pl.DeviceIdType.MESH


def adam_terms(step):
    bias_first = 1.0 - jnp.exp(step * jnp.float32(math.log(0.9)))
    bias_second = 1.0 - jnp.exp(step * jnp.float32(math.log(0.95)))
    return 1.0 / bias_first, 1.0 / bias_second


def kernel(
    line,
    heads,
    clip_total,
    step_ref,
    act_ref,
    vg_ref,
    master_ref,
    first_ref,
    second_ref,
    new_master_ref,
    new_first_ref,
    new_second_ref,
    rollout_ref,
    act,
    vg,
    acc,
    q_out,
    s_out,
    q_in,
    s_in,
    squares,
    norms,
    tally,
    w_in,
    m_in,
    v_in,
    w_out,
    m_out,
    v_out,
    update,
    in_sem,
    pair_send,
    pair_recv,
    load_sem,
    rs_send,
    near_recv,
    wide_recv,
    meet,
    norm_sem,
    store_sem,
    a2a_send,
    a2a_recv,
    spread_send,
    chain_recv,
    mate_recv,
):
    dpn = 2 * line
    dp = lax.axis_index("dp")
    mp = lax.axis_index("mp")
    z = dp // 2
    core = lax.rem(dp, 2)
    mate = dp + 1 - 2 * core
    tokens = act_ref.shape[0]
    rows = master_ref.shape[0]
    cols = master_ref.shape[1]
    head_cols = cols // heads
    tile = head_cols // 2
    half = rows // 2
    units = 4 * heads

    lower = z < line // 2
    at_end = (z == 0) | (z == line - 1)
    end = jnp.where(lower, 0, line - 1)
    mid = jnp.where(lower, 1, line - 2)
    far_mid = line - 1 - mid
    far_end = line - 1 - end
    toward = jnp.where(lower, 2, -2)
    ahead = dp + toward
    behind = jnp.where(at_end, dp, dp - toward)

    def peer(slot):
        return lax.rem(mp // 2 + slot // 2, heads // 2) * 2 + lax.rem(mp + slot % 2, 2)

    def source(slot):
        y = lax.rem(mp // 2 + heads // 2 - slot // 2, heads // 2)
        return y * 2 + lax.rem(mp + slot % 2, 2)

    barrier = pltpu.get_barrier_semaphore()
    pl.semaphore_signal(barrier, inc=1, device_id={"dp": mate}, device_id_type=MESH)
    pl.semaphore_signal(barrier, inc=1, device_id={"dp": ahead}, device_id_type=MESH)

    @pl.when(jnp.logical_not(at_end))
    def _():
        pl.semaphore_signal(barrier, inc=1, device_id={"dp": behind}, device_id_type=MESH)

    for slot in (1, 2):
        pl.semaphore_signal(barrier, inc=1, device_id={"mp": peer(slot)}, device_id_type=MESH)

    def own_act(dest):
        start = pl.multiple_of((dest * 2 + core) * rows, rows)
        return pltpu.make_async_copy(
            act_ref.at[:, pl.ds(start, rows)],
            act.at[dest, pl.ds(0, tokens)],
            in_sem.at[dest],
        )

    def head_lanes(slot):
        return pl.ds(pl.multiple_of(peer(slot) * head_cols, head_cols), head_cols)

    def chunk_lanes(k):
        at = peer(k // 2) * 2 + k % 2
        return pl.ds(pl.multiple_of(at * tile, tile), tile)

    def unit(k):
        return pl.ds(pl.multiple_of(k % 2 * half, half), half), chunk_lanes(k // 2)

    def own_vg(slot):
        at = head_lanes(slot)
        return pltpu.make_async_copy(
            vg_ref.at[:, at], vg.at[pl.ds(0, tokens), at], in_sem.at[line + slot]
        )

    def pair_act(dest, part=None):
        at = part or 0
        count = rows if part is None else half
        start = pl.multiple_of((dest * 2 + 1 - core) * rows + at * half, half)
        return pltpu.make_async_remote_copy(
            src_ref=act_ref.at[:, pl.ds(start, count)],
            dst_ref=act.at[dest, pl.ds(tokens, tokens), pl.ds(at * half, count)],
            send_sem=pair_send.at[0],
            recv_sem=pair_recv.at[line if part else dest],
            device_id={"dp": mate},
            device_id_type=MESH,
        )

    def pair_vg(slot, part=None):
        at = head_lanes(slot) if part is None else chunk_lanes(2 * slot + part)
        return pltpu.make_async_remote_copy(
            src_ref=vg_ref.at[:, at],
            dst_ref=vg.at[pl.ds(tokens, tokens), at],
            send_sem=pair_send.at[1],
            recv_sem=pair_recv.at[line + 1 + (heads if part else slot)],
            device_id={"dp": mate},
            device_id_type=MESH,
        )

    order = [
        far_end,
        jnp.where(at_end, far_mid, end),
        jnp.where(at_end, mid, far_mid),
        jnp.where(at_end, end, mid),
    ]
    own_act(order[0]).start()
    for slot in range(heads):
        own_vg(slot).start()
    for dest in order[1:]:
        own_act(dest).start()
    loads = [
        pltpu.make_async_copy(src, dst, load_sem.at[i])
        for i, (src, dst) in enumerate(
            ((master_ref, w_in), (first_ref, m_in), (second_ref, v_in))
        )
    ]
    with jax.named_scope("bar"):
        pl.semaphore_wait(barrier, jnp.where(at_end, 4, 5))
    for part in range(2):
        pair_act(order[0], part).start()
        pair_vg(0, part).start()
    for slot in range(1, heads):
        pair_vg(slot).start()
    for dest in order[1:]:
        pair_act(dest).start()
    for copy in loads:
        copy.start()

    def ready(dest):
        own_act(dest).wait()
        pair_act(dest).wait_recv()

    def ready_vg(slot):
        own_vg(slot).wait()
        pair_vg(slot).wait_recv()

    def multiply_unit(dest, part, k):
        at = chunk_lanes(k)
        here = slice(part * half, (part + 1) * half)
        acc[dest, here, at] = lax.dot_general(
            act[dest, :, here], vg[:, at], (((0,), (0,)), ((), ())), preferred_element_type=F32
        )

    def multiply(dest, slot):
        at = head_lanes(slot)
        acc[dest, :, at] = lax.dot_general(
            act[dest], vg[:, at], (((0,), (0,)), ((), ())), preferred_element_type=F32
        )

    def hop(dest, k, way, i, to):
        recv = (near_recv, wide_recv)[way]
        data = pltpu.make_async_remote_copy(
            src_ref=q_out.at[dest, k],
            dst_ref=q_in.at[way, dest, k],
            send_sem=rs_send.at[0, dest],
            recv_sem=recv.at[i],
            device_id={"dp": to},
            device_id_type=MESH,
        )
        scale = pltpu.make_async_remote_copy(
            src_ref=s_out.at[dest, k],
            dst_ref=s_in.at[way, dest, k],
            send_sem=rs_send.at[1, dest],
            recv_sem=recv.at[i],
            device_id={"dp": to},
            device_id_type=MESH,
        )
        return data, scale

    def take(dest, k, way, i):
        pltpu.make_async_copy(tally, tally, (near_recv, wide_recv)[way].at[i]).wait()
        top = s_in[way, dest, k] * (1.0 / LEVELS)
        got = q_in[way, dest, k].astype(jnp.int32).astype(F32)
        return acc[dest, *unit(k)] + got * top

    def give(total, dest, k, way, i, to):
        top = jnp.maximum(jnp.max(jnp.abs(total), axis=0, keepdims=True), 1e-30)
        s_out[dest, k] = top
        q_out[dest, k] = jnp.round(total * (LEVELS / top)).astype(jnp.int32).astype(jnp.int16)
        for copy in hop(dest, k, way, i, to):
            copy.start()

    def add_squares(total):
        squares[...] += jnp.sum((total * total).reshape(half // 8, 8, tile), axis=0)

    def place(i, first, second):
        dest = jnp.where(i < units, first, second)
        return dest, jnp.where(i < units, i, lax.rem(i + RES, units))

    squares[...] = jnp.zeros(squares.shape, F32)

    def hello(stage):
        slot = stage + 1
        pl.semaphore_signal(
            meet.at[stage], inc=1, device_id={"mp": peer(slot)}, device_id_type=MESH
        )

    def heard(stage):
        pl.semaphore_wait(meet.at[stage], 1)

    def send(i):
        dest, k = place(i, far_end, far_mid)
        dest = jnp.where(i < 2 * units, dest, mid)
        k = jnp.where(i < 2 * units, k, i - 2 * units)
        give(acc[dest, *unit(k)], dest, k, 0, i, ahead)

    @pl.when(at_end)
    def _():
        own_act(far_end).wait()
        own_vg(0).wait()
        for k in range(2):
            for part in range(2):
                with jax.named_scope(f"Ew{k}{part}"):
                    if k == 0:
                        pair_act(far_end, part).wait_recv()
                    if part == 0:
                        pair_vg(0, k).wait_recv()
                with jax.named_scope(f"Em{k}{part}"):
                    multiply_unit(far_end, part, k)
                    send(2 * k + part)

        for slot in range(1, heads):
            with jax.named_scope(f"Em{slot}"):
                ready_vg(slot)
                multiply(far_end, slot)
                for k in range(4):
                    send(4 * slot + k)

        with jax.named_scope("Erest"):
            ready(far_mid)

            @pl.loop(0, heads)
            def _(step):
                multiply(far_mid, lax.rem(step + RES // 4, heads))
                for k in range(4):
                    send(units + 4 * step + k)

            ready(mid)

            @pl.loop(0, heads)
            def _(slot):
                multiply(mid, slot)

            @pl.loop(2 * units, 2 * units + RES + EARLY)
            def _(i):
                send(i)

            ready(end)

            @pl.loop(0, heads)
            def _(slot):
                multiply(end, slot)

        @pl.loop(0, 2 * units - RES)
        def _(j):
            with jax.named_scope("Et"):
                dest, k = place(j, end, mid)
                total = take(dest, k, 1, j)
                add_squares(total)

                @pl.when(j < units)
                def _():
                    acc[dest, *unit(k)] = total

                @pl.when(j == 1)
                def _():
                    hello(0)

                @pl.when(j == units // 2)
                def _():
                    heard(0)
                    hello(1)

        heard(1)

    @pl.when(jnp.logical_not(at_end))
    def _():
        own_act(far_end).wait()
        own_vg(0).wait()
        for part in range(2):
            pair_act(far_end, part).wait_recv()
            pair_vg(0, part).wait_recv()
        for slot in range(heads):
            with jax.named_scope(f"Mm{slot}"):
                if slot:
                    ready_vg(slot)
                multiply(far_end, slot)
        for dest in order[1:]:
            ready(dest)

        def onward(j):
            dest, k = place(j, end, mid)
            total = take(dest, k, 1, j)

            @pl.when(j < 2 * units - RES)
            def _():
                give(total, dest, k, 1, j, behind)

            @pl.when(j >= units)
            def _():
                acc[dest, *unit(k)] = total

        @pl.loop(0, 2 * units)
        def _(i):
            with jax.named_scope("Mn"):
                dest, k = place(i, far_end, far_mid)
                give(take(dest, k, 0, i), dest, k, 1, i, ahead)

            @pl.when(i < 3 * heads)
            def _():
                dest = jnp.where(i < heads, end, jnp.where(i < 2 * heads, far_mid, mid))
                multiply(dest, lax.rem(i, heads))

            @pl.when(i >= LAG)
            def _():
                with jax.named_scope("Mf"):
                    onward(i - LAG)

            @pl.when(i == LAG + 1)
            def _():
                hello(0)

            @pl.when(i == LAG + units // 2)
            def _():
                heard(0)
                hello(1)

        @pl.loop(2 * units - LAG, 2 * units - RES)
        def _(j):
            with jax.named_scope("Mf"):
                onward(j)

        @pl.loop(0, RES)
        def _(k):
            with jax.named_scope("Mr"):
                onward(2 * units - RES + k)
                total = take(mid, k, 0, 2 * units + k)
                acc[mid, *unit(k)] = total
                add_squares(total)

        heard(1)

    me = dp * heads + mp
    norms[me] = jnp.sum(squares[...], axis=0, keepdims=True)

    def norm_to(step, slot):
        return pltpu.make_async_remote_copy(
            src_ref=norms.at[me],
            dst_ref=norms.at[me],
            send_sem=norm_sem.at[0],
            recv_sem=norm_sem.at[1],
            device_id={"dp": lax.rem(dp + step, dpn), "mp": lax.rem(mp + slot, heads)},
            device_id_type=MESH,
        )

    def taken(ref, sem):
        pltpu.make_async_copy(ref, ref, sem).wait()

    others = [(step, slot) for step in range(dpn) for slot in range(heads) if step + slot]
    with jax.named_scope("ns"):
        for step, slot in others:
            norm_to(step, slot).start()

    @pl.when(at_end)
    def _():
        @pl.loop(2 * units + RES + EARLY, 3 * units)
        def _(i):
            send(i)

    for copy in loads:
        copy.wait()
    with jax.named_scope("nw"):
        taken(norms.at[pl.ds(0, len(others))], norm_sem.at[1])
    square_sum = jnp.sum(jnp.sum(norms[...], axis=0), keepdims=True)
    factor = jnp.minimum(1.0, clip_total / (jnp.sqrt(square_sum) + 1e-06))
    step_count = jnp.full((1, 1), step_ref[0].astype(F32), F32)
    scale_first, scale_second = adam_terms(step_count)

    def block(owner, origin, part):
        start = (owner * dpn + origin) * rows + part * half
        return rollout_ref.at[pl.ds(pl.multiple_of(start, half), half)]

    def piece(head, part):
        return update.at[head, pl.ds(part * half, half)]

    def mine(part):
        return pltpu.make_async_copy(
            piece(mp, part), block(mp, dp, part), store_sem.at[3]
        )

    def to_head(slot, part):
        return pltpu.make_async_remote_copy(
            src_ref=piece(peer(slot), part),
            dst_ref=block(mp, dp, part),
            send_sem=a2a_send.at[0],
            recv_sem=a2a_recv.at[slot, part],
            device_id={"mp": peer(slot)},
            device_id_type=MESH,
        )

    def relay(ref, owner, at_z, part, send, recv, to):
        return pltpu.make_async_remote_copy(
            src_ref=ref,
            dst_ref=block(owner, at_z * 2 + core, part),
            send_sem=send,
            recv_sem=recv,
            device_id={"dp": to},
            device_id_type=MESH,
        )

    def send_ahead(ref, owner, at_z, part, sem=0):
        recv = chain_recv.at[at_z, owner, part]
        return relay(ref, owner, at_z, part, spread_send.at[sem], recv, ahead)

    def send_behind(ref, owner, at_z, part):
        recv = chain_recv.at[at_z, owner, part]
        return relay(ref, owner, at_z, part, spread_send.at[2], recv, behind)

    def send_mate(ref, owner, at_z, part):
        return relay(ref, owner, at_z, part, spread_send.at[3], mate_recv.at[0], mate)

    def spread(ref, owner, part):
        @pl.when(jnp.logical_not(at_end))
        def _():
            send_behind(ref, owner, z, part).start()

        send_ahead(ref, owner, z, part).start()
        send_mate(ref, owner, z, part).start()

    def from_ahead(at_z, slot, part):
        owner = source(slot)
        ref = block(owner, at_z * 2 + core, part)
        send_ahead(ref, owner, at_z, part).wait_recv()

        @pl.when(jnp.logical_not(at_end))
        def _():
            send_behind(ref, owner, at_z, part).start()

        send_mate(ref, owner, at_z, part).start()

    def from_behind(slot, part):
        owner = source(slot)
        ref = block(owner, end * 2 + core, part)
        send_ahead(ref, owner, end, part).wait_recv()
        send_ahead(ref, owner, end, part, 1).start()
        send_mate(ref, owner, end, part).start()

    def from_plane(slot, part):
        to_head(slot, part).wait_recv()
        spread(block(source(slot), dp, part), source(slot), part)

    slab = min(32, half)

    def step_rows(slot, part):
        lanes = head_lanes(slot)

        @pl.loop(0, half // slab)
        def _(r):
            at = pl.ds(pl.multiple_of(part * half + r * slab, slab), slab)
            clipped = acc[z, at, lanes] * factor
            weight = w_in[at, lanes]
            first = 0.9 * m_in[at, lanes] + 0.1 * clipped
            second = 0.95 * v_in[at, lanes] + 0.05 * clipped * clipped
            m_out[at, lanes] = first
            v_out[at, lanes] = second
            direction = (first * scale_first) / (
                jnp.sqrt(second * scale_second) + 1e-08
            ) + 0.1 * weight
            w_out[at, lanes] = weight - 0.01 * direction
            update[peer(slot), at, :] = direction.astype(jnp.bfloat16)

    def late(slot):
        @pl.when(jnp.logical_not(at_end))
        def _():
            @pl.loop(4 * slot, 4 * slot + 4)
            def _(k):
                acc[mid, *unit(k)] = take(mid, k, 0, 2 * units + k)

    work = [(slot, part) for slot in range(heads) for part in range(2)]
    for slot, part in work:
        with jax.named_scope(f"up{slot}{part}"):
            if part == 0 and 4 * slot >= RES:
                late(slot)
            step_rows(slot, part)
            if slot == 0:
                mine(part).start()
                spread(piece(mp, part), mp, part)
            else:
                to_head(slot, part).start()

    stores = [
        pltpu.make_async_copy(src, dst, store_sem.at[i])
        for i, (src, dst) in enumerate(
            ((w_out, new_master_ref), (m_out, new_first_ref), (v_out, new_second_ref))
        )
    ]
    for copy in stores:
        copy.start()

    @pl.when(at_end)
    def _():
        with jax.named_scope("Eaa"):
            for slot, part in work[2:]:
                from_plane(slot, part)
        for at_z in (mid, far_mid, far_end):
            with jax.named_scope("Efar"):
                for slot, part in work:
                    from_ahead(at_z, slot, part)

    @pl.when(jnp.logical_not(at_end))
    def _():
        for t, (slot, part) in enumerate(work[2:]):
            if t < 3:
                with jax.named_scope(f"Mah{t}"):
                    from_ahead(far_mid, *work[t])
            with jax.named_scope(f"Maa{t}"):
                from_plane(slot, part)
        for t in range(8):
            with jax.named_scope(f"Mfar{t}"):
                if t >= 3:
                    from_ahead(far_mid, *work[t])
                from_behind(*work[t])
        with jax.named_scope("Mfare"):
            for slot, part in work:
                from_ahead(far_end, slot, part)

    with jax.named_scope("tail"):
        plane = heads * rows
        taken(rollout_ref.at[pl.ds(0, line * plane)], mate_recv.at[0])
        taken(rollout_ref.at[pl.ds(0, line * plane)], spread_send.at[3])
        taken(rollout_ref.at[pl.ds(0, plane)], spread_send.at[0])

        @pl.when(jnp.logical_not(at_end))
        def _():
            taken(rollout_ref.at[pl.ds(0, plane)], spread_send.at[1])
            taken(rollout_ref.at[pl.ds(0, (line - 1) * plane)], spread_send.at[2])

        taken(update.at[pl.ds(0, heads - 1)], a2a_send.at[0])
        taken(norms.at[pl.ds(0, len(others))], norm_sem.at[0])
        taken(act.at[:, pl.ds(0, tokens)], pair_send.at[0])
        taken(vg.at[pl.ds(0, tokens)], pair_send.at[1])
        for i, ref in enumerate((q_out, s_out)):
            for dest in (far_end, far_mid):
                taken(ref.at[dest], rs_send.at[i, dest])

            @pl.when(at_end)
            def _():
                taken(ref.at[mid], rs_send.at[i, mid])

            @pl.when(jnp.logical_not(at_end))
            def _():
                taken(ref.at[end], rs_send.at[i, end])
                taken(ref.at[mid, pl.ds(RES, units - RES)], rs_send.at[i, mid])

        taken(update.at[0], store_sem.at[3])
        for copy in stores:
            copy.wait()


def settle(*refs):
    count = (len(refs) - 1) // 2
    sem = refs[-1]
    copies = []
    for i in range(count):
        source, place = refs[i], refs[count + i]
        piece = source.shape[0] // PIECES[i]
        for j in range(PIECES[i]):
            at = pl.ds(j * piece, piece)
            copies.append(
                pltpu.make_async_copy(source.at[at], place.at[at], sem.at[len(copies)])
            )
    for copy in copies:
        copy.start()
    for copy in copies:
        copy.wait()


def one_kernel(line, heads, activations, value_grad, master, first_moment, second_moment, step_count):
    rows, cols = master.shape
    tokens = activations.shape[0]
    tile = cols // heads // 2
    units = 4 * heads
    dpn = 2 * line
    clip_total = 0.5 * math.sqrt(rows * dpn * heads * cols)
    hbm = pl.BlockSpec(memory_space=pl.ANY)
    owned = jax.ShapeDtypeStruct((rows, cols), F32)
    wide = pltpu.VMEM((rows, cols), F32)
    dma = pltpu.SemaphoreType.DMA
    results = pl.pallas_call(
        functools.partial(kernel, line, heads, clip_total),
        out_shape=(
            owned,
            owned,
            owned,
            jax.ShapeDtypeStruct((rows * dpn * heads, cols // heads), jnp.bfloat16),
        ),
        in_specs=[pl.BlockSpec(memory_space=pltpu.SMEM)]
        + [hbm] * 5,
        out_specs=(hbm,) * 4,
        scratch_shapes=[
            pltpu.VMEM((line, 2 * tokens, rows), jnp.bfloat16),
            pltpu.VMEM((2 * tokens, cols), jnp.bfloat16),
            pltpu.VMEM((line, rows, cols), F32),
            pltpu.VMEM((line, units, rows // 2, tile), jnp.int16),
            pltpu.VMEM((line, units, 1, tile), F32),
            pltpu.VMEM((2, line, units, rows // 2, tile), jnp.int16),
            pltpu.VMEM((2, line, units, 1, tile), F32),
            pltpu.VMEM((8, tile), F32),
            pltpu.VMEM((dpn * heads, 1, tile), F32),
            pltpu.VMEM((rows // 4 + 1, 1, tile), F32),
            wide,
            wide,
            wide,
            wide,
            wide,
            wide,
            pltpu.VMEM((heads, rows, cols // heads), jnp.bfloat16),
            dma((line + heads,)),
            dma((2,)),
            dma((line + heads + 2,)),
            dma((3,)),
            dma((2, line)),
            dma((3 * units,)),
            dma((2 * units,)),
            pltpu.SemaphoreType.REGULAR((2,)),
            dma((2,)),
            dma((4,)),
            dma((1,)),
            dma((heads, 2)),
            dma((4,)),
            dma((line, heads, 2)),
            dma((1,)),
        ],
        compiler_params=pltpu.CompilerParams(
            collective_id=0, has_side_effects=True, vmem_limit_bytes=28 * 1024 * 1024
        ),
    )(
        step_count,
        *(
            pltpu.with_memory_space_constraint(x, pltpu.HBM)
            for x in (activations, value_grad, master, first_moment, second_moment)
        ),
    )
    shapes = tuple(jax.ShapeDtypeStruct(x.shape, x.dtype) for x in results)
    return pl.pallas_call(
        settle,
        out_shape=shapes,
        in_specs=[hbm] * 4,
        out_specs=(hbm,) * 4,
        scratch_shapes=[dma((sum(PIECES),))],
        compiler_params=pltpu.CompilerParams(vmem_limit_bytes=4 * 1024 * 1024),
    )(*(pltpu.with_memory_space_constraint(x, pltpu.VMEM) for x in results))


def plain(activations, value_grad, master, first_moment, second_moment, step_count):
    own_rows, cols = master.shape
    grad = lax.psum_scatter(
        lax.dot_general(
            activations, value_grad, (((0,), (0,)), ((), ())), preferred_element_type=F32
        ),
        "dp",
        scatter_dimension=0,
        tiled=True,
    )
    square_sum = lax.psum(jnp.sum(grad * grad), ("dp", "mp"))
    head_count = lax.axis_size("mp")
    clip_total = 0.5 * math.sqrt(own_rows * lax.axis_size("dp") * head_count * cols)
    factor = jnp.minimum(jnp.float32(1.0), clip_total / (jnp.sqrt(square_sum) + 1e-06))
    clipped = factor * grad
    new_first = 0.9 * first_moment + 0.1 * clipped
    new_second = 0.95 * second_moment + 0.05 * clipped * clipped
    scale_first, scale_second = adam_terms(step_count[0].astype(F32))
    direction = new_first * scale_first / (jnp.sqrt(new_second * scale_second) + 1e-08) + 0.1 * master
    new_master = master - 0.01 * direction
    update = direction.astype(jnp.bfloat16)
    received = lax.all_to_all(update, "mp", split_axis=1, concat_axis=0, tiled=True)
    stacked = received.reshape(head_count, own_rows, received.shape[1])
    gathered = lax.all_gather(stacked, "dp", axis=1, tiled=True)
    return (new_master, new_first, new_second, gathered.reshape(-1, gathered.shape[2]))


def solution(mesh):
    dpn, heads = mesh.shape["dp"], mesh.shape["mp"]

    def on_device(*args):
        rows, cols = args[2].shape
        if dpn == 8 and heads == 4 and rows % 64 == 0 and (cols // heads) % 256 == 0:
            return one_kernel(dpn // 2, heads, *args)
        return plain(*args)

    in_specs = (
        P("dp", "mp"),
        P("dp", None),
        P(("mp", "dp"), None),
        P(("mp", "dp"), None),
        P(("mp", "dp"), None),
        P(),
    )
    out_specs = (P(("mp", "dp"), None), P(("mp", "dp"), None), P(("mp", "dp"), None), P(None, "mp"))
    return jax.shard_map(
        on_device, mesh=mesh, in_specs=in_specs, out_specs=out_specs, check_vma=False
    )
```

time: 90.8 us -> 81.8 us (0.901)
  Pallas kernels: 89.3 us -> 80.4 us
    pallas_call x1, Pallas kernels: 86.3 us -> 77.3 us  [one_kernel(): pl.pallas_call(functools.partial(kernel, line, heads, clip_total), out_sh...]
where the time goes in v2:
time: 81.8 us; the launch traced here: 81.7 us
  Pallas kernels  80.4 us (98%)
  between operations  1.29 us (2%)
    pallas_call x1, Pallas kernels, one_kernel(): pl.pallas_call(functools.partial(kernel, line, heads, clip_total), out_sh...  77.3 us
    pallas_call x1, Pallas kernels, one_kernel(): pl.pallas_call(settle, out_shape=shapes, in_specs=[hbm] * 4, out_specs=(h...  3.05 us

profile of v2, /device:TPU:0, one launch (start us, length us, event | category | flops | bytes accessed | tf_op | source)
XLA Modules:
  0.0 81.7 jit_solution(3335235999745446141)
XLA Ops:
  1.3 77.3 %shard_map.93 = (f32[256,1024]{1,0:T(8,128)S(1)}, f32[256,1024]{1,0:T(8,128)S(1)}, f32[256,1024]{1,0:T(8,128)S(1)}, bf16[8192,256]{1,0:T(8,128)(2,1)S(1)}) custom-call(s32[1]{0:T(128)S(6)} %copy.10.step_ref, bf16[512,2048]{1,0:T(8,128)(2,1)} %act_ref.1, bf16[512,1024]{1,0:T(8,128)(2,1)} %vg_ref.1, f32[256,1024]{1,0:T(8,128)} %master_ref.1, ...), custom_call_target="tpu_custom_call" | custom-call | tf_op jit(solution)/shard_map/pallas_call | solution.py:652
  78.6 3.0 %shard_map.94 = (f32[256,1024]{1,0:T(8,128)}, f32[256,1024]{1,0:T(8,128)}, f32[256,1024]{1,0:T(8,128)}, bf16[8192,256]{1,0:T(8,128)(2,1)}) custom-call(f32[256,1024]{1,0:T(8,128)S(1)} %get-tuple-element.8.refs_0_, f32[256,1024]{1,0:T(8,128)S(1)} %get-tuple-element.9.refs_1_, f32[256,1024]{1,0:T(8,128)S(1)} %get-tuple-element.10.refs_2_, ...), custom_call_target="tpu_custom_call" | custom-call | tf_op jit(solution)/shard_map/pallas_call | solution.py:708

commit v3 on v2

--- a/solution.py
+++ b/solution.py
@@ -14,6 +14,8 @@
 RES = 4
 LAG = 4
 EARLY = 4
+SHADOW = 3
+BEFORE = 5
 MESH = pl.DeviceIdType.MESH
 
 
@@ -54,6 +56,8 @@
     m_out,
     v_out,
     update,
+    shadow_q,
+    shadow_s,
     in_sem,
     pair_send,
     pair_recv,
@@ -63,11 +67,8 @@
     wide_recv,
     meet,
     norm_sem,
-    store_sem,
+    shadow_sem,
     a2a_send,
-    a2a_recv,
-    spread_send,
-    chain_recv,
     mate_recv,
 ):
     dpn = 2 * line
@@ -83,6 +84,7 @@
     tile = head_cols // 2
     half = rows // 2
     units = 4 * heads
+    blocks = 2 * heads
 
     lower = z < line // 2
     at_end = (z == 0) | (z == line - 1)
@@ -177,6 +179,8 @@
             ((master_ref, w_in), (first_ref, m_in), (second_ref, v_in))
         )
     ]
+    for copy in loads:
+        copy.start()
     with jax.named_scope("bar"):
         pl.semaphore_wait(barrier, jnp.where(at_end, 4, 5))
     for part in range(2):
@@ -186,8 +190,6 @@
         pair_vg(slot).start()
     for dest in order[1:]:
         pair_act(dest).start()
-    for copy in loads:
-        copy.start()
 
     def ready(dest):
         own_act(dest).wait()
@@ -230,16 +232,22 @@
         )
         return data, scale
 
+    def arrived(way, i):
+        pltpu.make_async_copy(tally, tally, (near_recv, wide_recv)[way].at[i]).wait()
+
     def take(dest, k, way, i):
-        pltpu.make_async_copy(tally, tally, (near_recv, wide_recv)[way].at[i]).wait()
-        top = s_in[way, dest, k] * (1.0 / LEVELS)
-        got = q_in[way, dest, k].astype(jnp.int32).astype(F32)
-        return acc[dest, *unit(k)] + got * top
+        arrived(way, i)
+        return acc[dest, *unit(k)] + decode(q_in[way, dest, k], s_in[way, dest, k])
+
+    def code(total):
+        top = jnp.maximum(jnp.max(jnp.abs(total), axis=0, keepdims=True), 1e-30)
+        return jnp.round(total * (LEVELS / top)).astype(jnp.int32).astype(jnp.int16), top
+
+    def decode(got, top):
+        return got.astype(jnp.int32).astype(F32) * (top * (1.0 / LEVELS))
 
     def give(total, dest, k, way, i, to):
-        top = jnp.maximum(jnp.max(jnp.abs(total), axis=0, keepdims=True), 1e-30)
-        s_out[dest, k] = top
-        q_out[dest, k] = jnp.round(total * (LEVELS / top)).astype(jnp.int32).astype(jnp.int16)
+        q_out[dest, k], s_out[dest, k] = code(total)
         for copy in hop(dest, k, way, i, to):
             copy.start()
 
@@ -249,6 +257,25 @@
     def place(i, first, second):
         dest = jnp.where(i < units, first, second)
         return dest, jnp.where(i < units, i, lax.rem(i + RES, units))
+
+    def shadowed(k):
+        return k // 4 * 2 + k % 2 >= blocks - SHADOW
+
+    def lend(first, last):
+        for at in range(first, last):
+            t, i = blocks - SHADOW + at // 3, at % 3
+            here = slice(t % 2 * half, (t % 2 + 1) * half)
+            value = (m_in, v_in, w_in)[i][here, head_lanes(t // 2)]
+            shadow_q[i, at // 3], shadow_s[i, at // 3] = code(value)
+            for j, ref in enumerate((shadow_q, shadow_s)):
+                pltpu.make_async_remote_copy(
+                    src_ref=ref.at[i, at // 3],
+                    dst_ref=ref.at[i, at // 3],
+                    send_sem=shadow_sem.at[j],
+                    recv_sem=shadow_sem.at[2 + j],
+                    device_id={"dp": behind},
+                    device_id_type=MESH,
+                ).start()
 
     squares[...] = jnp.zeros(squares.shape, F32)
 
@@ -293,10 +320,12 @@
             ready(far_mid)
 
             @pl.loop(0, heads)
-            def _(step):
-                multiply(far_mid, lax.rem(step + RES // 4, heads))
-                for k in range(4):
-                    send(units + 4 * step + k)
+            def _(slot):
+                multiply(far_mid, slot)
+
+            @pl.loop(units, 2 * units)
+            def _(i):
+                send(i)
 
             ready(mid)
 
@@ -325,6 +354,12 @@
                 def _():
                     acc[dest, *unit(k)] = total
 
+                @pl.when((j >= units) & shadowed(k))
+                def _():
+                    q, top = code(total)
+                    q_out[mid, k], s_out[mid, k] = q, top
+                    q_in[0, mid, k], s_in[0, mid, k] = q, top
+
                 @pl.when(j == 1)
                 def _():
                     hello(0)
@@ -338,6 +373,10 @@
 
     @pl.when(jnp.logical_not(at_end))
     def _():
+        with jax.named_scope("Ml"):
+            for copy in loads:
+                copy.wait()
+            lend(0, BEFORE)
         own_act(far_end).wait()
         own_vg(0).wait()
         for part in range(2):
@@ -428,10 +467,25 @@
     def _():
         @pl.loop(2 * units + RES + EARLY, 3 * units)
         def _(i):
-            send(i)
-
-    for copy in loads:
-        copy.wait()
+            k = i - 2 * units
+
+            @pl.when(shadowed(k))
+            def _():
+                for copy in hop(mid, k, 0, i, ahead):
+                    copy.start()
+
+            @pl.when(jnp.logical_not(shadowed(k)))
+            def _():
+                send(i)
+
+        for copy in loads:
+            copy.wait()
+
+    @pl.when(jnp.logical_not(at_end))
+    def _():
+        with jax.named_scope("Ml2"):
+            lend(BEFORE, 3 * SHADOW)
+
     with jax.named_scope("nw"):
         taken(norms.at[pl.ds(0, len(others))], norm_sem.at[1])
     square_sum = jnp.sum(jnp.sum(norms[...], axis=0), keepdims=True)
@@ -444,11 +498,11 @@
         return rollout_ref.at[pl.ds(pl.multiple_of(start, half), half)]
 
     def piece(head, part):
-        return update.at[head, pl.ds(part * half, half)]
+        return update.at[head * 2 + part]
 
     def mine(part):
         return pltpu.make_async_copy(
-            piece(mp, part), block(mp, dp, part), store_sem.at[3]
+            piece(mp, part), block(mp, dp, part), in_sem.at[line + 3]
         )
 
     def to_head(slot, part):
@@ -456,8 +510,19 @@
             src_ref=piece(peer(slot), part),
             dst_ref=block(mp, dp, part),
             send_sem=a2a_send.at[0],
-            recv_sem=a2a_recv.at[slot, part],
+            recv_sem=near_recv.at[slot * 2 + part],
             device_id={"mp": peer(slot)},
+            device_id_type=MESH,
+        )
+
+    def to_shadow(at):
+        t = blocks - SHADOW + at
+        return pltpu.make_async_remote_copy(
+            src_ref=update.at[blocks + at],
+            dst_ref=block(mp, mid * 2 + core, t % 2),
+            send_sem=shadow_sem.at[0],
+            recv_sem=near_recv.at[blocks + at],
+            device_id={"mp": peer(t // 2)},
             device_id_type=MESH,
         )
 
@@ -472,20 +537,22 @@
         )
 
     def send_ahead(ref, owner, at_z, part, sem=0):
-        recv = chain_recv.at[at_z, owner, part]
-        return relay(ref, owner, at_z, part, spread_send.at[sem], recv, ahead)
+        recv = wide_recv.at[(at_z * heads + owner) * 2 + part]
+        return relay(ref, owner, at_z, part, in_sem.at[sem], recv, ahead)
 
     def send_behind(ref, owner, at_z, part):
-        recv = chain_recv.at[at_z, owner, part]
-        return relay(ref, owner, at_z, part, spread_send.at[2], recv, behind)
+        recv = wide_recv.at[(at_z * heads + owner) * 2 + part]
+        return relay(ref, owner, at_z, part, in_sem.at[2], recv, behind)
 
     def send_mate(ref, owner, at_z, part):
-        return relay(ref, owner, at_z, part, spread_send.at[3], mate_recv.at[0], mate)
-
-    def spread(ref, owner, part):
-        @pl.when(jnp.logical_not(at_end))
-        def _():
-            send_behind(ref, owner, z, part).start()
+        return relay(ref, owner, at_z, part, in_sem.at[3], mate_recv.at[0], mate)
+
+    def spread(ref, owner, part, back=True):
+        if back:
+
+            @pl.when(jnp.logical_not(at_end))
+            def _():
+                send_behind(ref, owner, z, part).start()
 
         send_ahead(ref, owner, z, part).start()
         send_mate(ref, owner, z, part).start()
@@ -510,7 +577,14 @@
 
     def from_plane(slot, part):
         to_head(slot, part).wait_recv()
-        spread(block(source(slot), dp, part), source(slot), part)
+        back = slot * 2 + part < blocks - SHADOW
+        spread(block(source(slot), dp, part), source(slot), part, back)
+
+    def from_shadow(at):
+        t = blocks - SHADOW + at
+        owner = source(t // 2)
+        to_shadow(at).wait_recv()
+        send_mate(block(owner, mid * 2 + core, t % 2), owner, mid, t % 2).start()
 
     slab = min(32, half)
 
@@ -530,21 +604,55 @@
                 jnp.sqrt(second * scale_second) + 1e-08
             ) + 0.1 * weight
             w_out[at, lanes] = weight - 0.01 * direction
-            update[peer(slot), at, :] = direction.astype(jnp.bfloat16)
+            here = pl.ds(pl.multiple_of(r * slab, slab), slab)
+            update[peer(slot) * 2 + part, here, :] = direction.astype(jnp.bfloat16)
+
+    def shadow_rows(at):
+        t = blocks - SHADOW + at
+        slot, part = t // 2, t % 2
+        to = jnp.where(at_end, blocks + at, peer(slot) * 2 + part)
+
+        @pl.loop(0, half // slab)
+        def _(r):
+            here = pl.ds(pl.multiple_of(r * slab, slab), slab)
+            for c in range(2):
+                k = 4 * slot + 2 * c + part
+                lanes = slice(c * tile, (c + 1) * tile)
+                first, second, weight = (
+                    decode(shadow_q[i, at, here, lanes], shadow_s[i, at, :, lanes])
+                    for i in range(3)
+                )
+                clipped = decode(q_in[0, mid, k, here, :], s_in[0, mid, k]) * factor
+                first = 0.9 * first + 0.1 * clipped
+                second = 0.95 * second + 0.05 * clipped * clipped
+                direction = (first * scale_first) / (
+                    jnp.sqrt(second * scale_second) + 1e-08
+                ) + 0.1 * weight
+                update[to, here, lanes] = direction.astype(jnp.bfloat16)
 
     def late(slot):
         @pl.when(jnp.logical_not(at_end))
         def _():
-            @pl.loop(4 * slot, 4 * slot + 4)
-            def _(k):
-                acc[mid, *unit(k)] = take(mid, k, 0, 2 * units + k)
+            for k in range(max(4 * slot, RES), 4 * slot + 4):
+                if shadowed(k):
+                    arrived(0, 2 * units + k)
+                    acc[mid, *unit(k)] = decode(q_in[0, mid, k], s_in[0, mid, k])
+                else:
+                    acc[mid, *unit(k)] = take(mid, k, 0, 2 * units + k)
 
     work = [(slot, part) for slot in range(heads) for part in range(2)]
     for slot, part in work:
         with jax.named_scope(f"up{slot}{part}"):
-            if part == 0 and 4 * slot >= RES:
+            at = slot * 2 + part - (blocks - SHADOW)
+            if part == 0 and 4 * slot + 4 > RES:
                 late(slot)
             step_rows(slot, part)
+            if at >= 0:
+
+                @pl.when(jnp.logical_not(at_end))
+                def _():
+                    shadow_rows(at)
+
             if slot == 0:
                 mine(part).start()
                 spread(piece(mp, part), mp, part)
@@ -552,7 +660,7 @@
                 to_head(slot, part).start()
 
     stores = [
-        pltpu.make_async_copy(src, dst, store_sem.at[i])
+        pltpu.make_async_copy(src, dst, in_sem.at[line + i])
         for i, (src, dst) in enumerate(
             ((w_out, new_master_ref), (m_out, new_first_ref), (v_out, new_second_ref))
         )
@@ -562,10 +670,20 @@
 
     @pl.when(at_end)
     def _():
+        with jax.named_scope("Es"):
+            for j, ref in enumerate((shadow_q, shadow_s)):
+                taken(ref, shadow_sem.at[2 + j])
+            for at in range(SHADOW):
+                shadow_rows(at)
+                to_shadow(at).start()
         with jax.named_scope("Eaa"):
             for slot, part in work[2:]:
                 from_plane(slot, part)
-        for at_z in (mid, far_mid, far_end):
+            for slot, part in work[: blocks - SHADOW]:
+                from_ahead(mid, slot, part)
+            for at in range(SHADOW):
+                from_shadow(at)
+        for at_z in (far_mid, far_end):
             with jax.named_scope("Efar"):
                 for slot, part in work:
                     from_ahead(at_z, slot, part)
@@ -590,15 +708,22 @@
     with jax.named_scope("tail"):
         plane = heads * rows
         taken(rollout_ref.at[pl.ds(0, line * plane)], mate_recv.at[0])
-        taken(rollout_ref.at[pl.ds(0, line * plane)], spread_send.at[3])
-        taken(rollout_ref.at[pl.ds(0, plane)], spread_send.at[0])
+        taken(rollout_ref.at[pl.ds(0, line * plane)], in_sem.at[3])
+        taken(rollout_ref.at[pl.ds(0, plane)], in_sem.at[0])
 
         @pl.when(jnp.logical_not(at_end))
         def _():
-            taken(rollout_ref.at[pl.ds(0, plane)], spread_send.at[1])
-            taken(rollout_ref.at[pl.ds(0, (line - 1) * plane)], spread_send.at[2])
-
-        taken(update.at[pl.ds(0, heads - 1)], a2a_send.at[0])
+            taken(rollout_ref.at[pl.ds(0, plane)], in_sem.at[1])
+            back = (line - 1) * plane - SHADOW * half
+            taken(rollout_ref.at[pl.ds(0, back)], in_sem.at[2])
+            for j, ref in enumerate((shadow_q, shadow_s)):
+                taken(ref, shadow_sem.at[j])
+
+        @pl.when(at_end)
+        def _():
+            taken(update.at[pl.ds(0, SHADOW)], shadow_sem.at[0])
+
+        taken(update.at[pl.ds(0, blocks - 2)], a2a_send.at[0])
         taken(norms.at[pl.ds(0, len(others))], norm_sem.at[0])
         taken(act.at[:, pl.ds(0, tokens)], pair_send.at[0])
         taken(vg.at[pl.ds(0, tokens)], pair_send.at[1])
@@ -615,7 +740,7 @@
                 taken(ref.at[end], rs_send.at[i, end])
                 taken(ref.at[mid, pl.ds(RES, units - RES)], rs_send.at[i, mid])
 
-        taken(update.at[0], store_sem.at[3])
+        taken(update.at[pl.ds(0, 2)], in_sem.at[line + 3])
         for copy in stores:
             copy.wait()
 
@@ -677,7 +802,9 @@
             wide,
             wide,
             wide,
-            pltpu.VMEM((heads, rows, cols // heads), jnp.bfloat16),
+            pltpu.VMEM((2 * heads + SHADOW, rows // 2, 2 * tile), jnp.bfloat16),
+            pltpu.VMEM((3, SHADOW, rows // 2, 2 * tile), jnp.int16),
+            pltpu.VMEM((3, SHADOW, 1, 2 * tile), F32),
             dma((line + heads,)),
             dma((2,)),
             dma((line + heads + 2,)),
@@ -689,9 +816,6 @@
             dma((2,)),
             dma((4,)),
             dma((1,)),
-            dma((heads, 2)),
-            dma((4,)),
-            dma((line, heads, 2)),
             dma((1,)),
         ],
         compiler_params=pltpu.CompilerParams(

time: 81.8 us -> 78.3 us (0.957)
  Pallas kernels: 80.4 us -> 76.9 us
    pallas_call x1, Pallas kernels: 77.3 us -> 73.8 us  [one_kernel(): pl.pallas_call(functools.partial(kernel, line, heads, clip_total), out_sh...]
where the time goes in v3:
time: 78.3 us; the launch traced here: 78.2 us
  Pallas kernels  76.9 us (98%)
  between operations  1.29 us (2%)
    pallas_call x1, Pallas kernels, one_kernel(): pl.pallas_call(functools.partial(kernel, line, heads, clip_total), out_sh...  73.8 us
    pallas_call x1, Pallas kernels, one_kernel(): pl.pallas_call(settle, out_shape=shapes, in_specs=[hbm] * 4, out_specs=(h...  3.05 us

profile of v3, /device:TPU:0, one launch (start us, length us, event | category | flops | bytes accessed | tf_op | source)
XLA Modules:
  0.0 78.2 jit_solution(5701730402883894875)
XLA Ops:
  1.3 73.8 %shard_map.93 = (f32[256,1024]{1,0:T(8,128)S(1)}, f32[256,1024]{1,0:T(8,128)S(1)}, f32[256,1024]{1,0:T(8,128)S(1)}, bf16[8192,256]{1,0:T(8,128)(2,1)S(1)}) custom-call(s32[1]{0:T(128)S(6)} %copy.10.step_ref, bf16[512,2048]{1,0:T(8,128)(2,1)} %act_ref.1, bf16[512,1024]{1,0:T(8,128)(2,1)} %vg_ref.1, f32[256,1024]{1,0:T(8,128)} %master_ref.1, ...), custom_call_target="tpu_custom_call" | custom-call | tf_op jit(solution)/shard_map/pallas_call | solution.py:777
  75.1 3.0 %shard_map.94 = (f32[256,1024]{1,0:T(8,128)}, f32[256,1024]{1,0:T(8,128)}, f32[256,1024]{1,0:T(8,128)}, bf16[8192,256]{1,0:T(8,128)(2,1)}) custom-call(f32[256,1024]{1,0:T(8,128)S(1)} %get-tuple-element.8.refs_0_, f32[256,1024]{1,0:T(8,128)S(1)} %get-tuple-element.9.refs_1_, f32[256,1024]{1,0:T(8,128)S(1)} %get-tuple-element.10.refs_2_, ...), custom_call_target="tpu_custom_call" | custom-call | tf_op jit(solution)/shard_map/pallas_call | solution.py:832

commit v4 on v3

--- a/solution.py
+++ b/solution.py
@@ -11,11 +11,13 @@
 F32 = jnp.float32
 LEVELS = 32760.0
 PIECES = (1, 1, 1, 4)
-RES = 4
-LAG = 4
-EARLY = 4
+RES = 5
+LAG = 5
+EARLY = 3
 SHADOW = 3
-BEFORE = 5
+LENT = (5, 7)
+ROOT_MID = (1.0 + math.sqrt(0.05)) / 2
+ROOT_SPAN = (1.0 - math.sqrt(0.05)) / 2
 MESH = pl.DeviceIdType.MESH
 
 
@@ -179,13 +181,16 @@
             ((master_ref, w_in), (first_ref, m_in), (second_ref, v_in))
         )
     ]
-    for copy in loads:
-        copy.start()
     with jax.named_scope("bar"):
         pl.semaphore_wait(barrier, jnp.where(at_end, 4, 5))
     for part in range(2):
         pair_act(order[0], part).start()
         pair_vg(0, part).start()
+    @pl.when(jnp.logical_not(at_end))
+    def _():
+        for copy in loads:
+            copy.start()
+
     for slot in range(1, heads):
         pair_vg(slot).start()
     for dest in order[1:]:
@@ -199,12 +204,17 @@
         own_vg(slot).wait()
         pair_vg(slot).wait_recv()
 
-    def multiply_unit(dest, part, k):
+    def multiply_unit(dest, part, k, mates):
         at = chunk_lanes(k)
         here = slice(part * half, (part + 1) * half)
-        acc[dest, here, at] = lax.dot_general(
-            act[dest, :, here], vg[:, at], (((0,), (0,)), ((), ())), preferred_element_type=F32
-        )
+        whose = slice(mates * tokens, (mates + 1) * tokens)
+        product = lax.dot_general(
+            act[dest, whose, here],
+            vg[whose, at],
+            (((0,), (0,)), ((), ())),
+            preferred_element_type=F32,
+        )
+        acc[dest, here, at] = acc[dest, here, at] + product if mates else product
 
     def multiply(dest, slot):
         at = head_lanes(slot)
@@ -263,14 +273,21 @@
 
     def lend(first, last):
         for at in range(first, last):
-            t, i = blocks - SHADOW + at // 3, at % 3
+            n, i = at // 3, at % 3
+            t = blocks - SHADOW + n
             here = slice(t % 2 * half, (t % 2 + 1) * half)
-            value = (m_in, v_in, w_in)[i][here, head_lanes(t // 2)]
-            shadow_q[i, at // 3], shadow_s[i, at // 3] = code(value)
-            for j, ref in enumerate((shadow_q, shadow_s)):
+            value = (m_in, w_in, v_in)[i][here, head_lanes(t // 2)]
+            refs = [shadow_q]
+            if i < 2:
+                shadow_q[i, n], shadow_s[i, n] = code(value)
+                refs.append(shadow_s)
+            else:
+                root = (jnp.sqrt(value) - ROOT_MID) * (LEVELS / ROOT_SPAN)
+                shadow_q[i, n] = jnp.round(root).astype(jnp.int32).astype(jnp.int16)
+            for j, ref in enumerate(refs):
                 pltpu.make_async_remote_copy(
-                    src_ref=ref.at[i, at // 3],
-                    dst_ref=ref.at[i, at // 3],
+                    src_ref=ref.at[i, n],
+                    dst_ref=ref.at[i, n],
                     send_sem=shadow_sem.at[j],
                     recv_sem=shadow_sem.at[2 + j],
                     device_id={"dp": behind},
@@ -298,6 +315,9 @@
     def _():
         own_act(far_end).wait()
         own_vg(0).wait()
+        for k in range(2):
+            for part in range(2):
+                multiply_unit(far_end, part, k, 0)
         for k in range(2):
             for part in range(2):
                 with jax.named_scope(f"Ew{k}{part}"):
@@ -306,7 +326,7 @@
                     if part == 0:
                         pair_vg(0, k).wait_recv()
                 with jax.named_scope(f"Em{k}{part}"):
-                    multiply_unit(far_end, part, k)
+                    multiply_unit(far_end, part, k, 1)
                     send(2 * k + part)
 
         for slot in range(1, heads):
@@ -316,6 +336,8 @@
                 for k in range(4):
                     send(4 * slot + k)
 
+        for copy in loads:
+            copy.start()
         with jax.named_scope("Erest"):
             ready(far_mid)
 
@@ -376,7 +398,7 @@
         with jax.named_scope("Ml"):
             for copy in loads:
                 copy.wait()
-            lend(0, BEFORE)
+            lend(0, LENT[0])
         own_act(far_end).wait()
         own_vg(0).wait()
         for part in range(2):
@@ -432,6 +454,8 @@
             with jax.named_scope("Mf"):
                 onward(j)
 
+        lend(*LENT)
+
         @pl.loop(0, RES)
         def _(k):
             with jax.named_scope("Mr"):
@@ -445,23 +469,29 @@
     me = dp * heads + mp
     norms[me] = jnp.sum(squares[...], axis=0, keepdims=True)
 
-    def norm_to(step, slot):
+    def norm_to(at_z, other, slot):
         return pltpu.make_async_remote_copy(
             src_ref=norms.at[me],
             dst_ref=norms.at[me],
             send_sem=norm_sem.at[0],
             recv_sem=norm_sem.at[1],
-            device_id={"dp": lax.rem(dp + step, dpn), "mp": lax.rem(mp + slot, heads)},
+            device_id={"dp": at_z * 2 + lax.rem(core + other, 2), "mp": peer(slot)},
             device_id_type=MESH,
         )
 
     def taken(ref, sem):
         pltpu.make_async_copy(ref, ref, sem).wait()
 
-    others = [(step, slot) for step in range(dpn) for slot in range(heads) if step + slot]
+    others = [
+        (at_z, other, slot)
+        for i, at_z in enumerate((far_end, far_mid, jnp.where(at_end, mid, end), z))
+        for slot in range(heads - 1, -1, -1)
+        for other in (1, 0)
+        if i < 3 or other or slot
+    ]
     with jax.named_scope("ns"):
-        for step, slot in others:
-            norm_to(step, slot).start()
+        for at in others:
+            norm_to(*at).start()
 
     @pl.when(at_end)
     def _():
@@ -484,7 +514,7 @@
     @pl.when(jnp.logical_not(at_end))
     def _():
         with jax.named_scope("Ml2"):
-            lend(BEFORE, 3 * SHADOW)
+            lend(LENT[1], 3 * SHADOW)
 
     with jax.named_scope("nw"):
         taken(norms.at[pl.ds(0, len(others))], norm_sem.at[1])
@@ -557,6 +587,28 @@
         send_ahead(ref, owner, z, part).start()
         send_mate(ref, owner, z, part).start()
 
+    def spread_slab(r):
+        here = pl.ds(r * slab, slab)
+        start = pl.multiple_of((mp * dpn + dp) * rows + r * slab, slab)
+        recv = wide_recv.at[(z * heads + mp) * 2]
+
+        def copy(i, recv, to):
+            return pltpu.make_async_remote_copy(
+                src_ref=update.at[mp * 2, here],
+                dst_ref=rollout_ref.at[pl.ds(start, slab)],
+                send_sem=in_sem.at[i],
+                recv_sem=recv,
+                device_id={"dp": to},
+                device_id_type=MESH,
+            )
+
+        @pl.when(jnp.logical_not(at_end))
+        def _():
+            copy(2, recv, behind).start()
+
+        copy(0, recv, ahead).start()
+        copy(3, mate_recv.at[0], mate).start()
+
     def from_ahead(at_z, slot, part):
         owner = source(slot)
         ref = block(owner, at_z * 2 + core, part)
@@ -588,10 +640,10 @@
 
     slab = min(32, half)
 
-    def step_rows(slot, part):
+    def step_rows(slot, part, first=0, last=half // slab):
         lanes = head_lanes(slot)
 
-        @pl.loop(0, half // slab)
+        @pl.loop(first, last)
         def _(r):
             at = pl.ds(pl.multiple_of(part * half + r * slab, slab), slab)
             clipped = acc[z, at, lanes] * factor
@@ -618,10 +670,13 @@
             for c in range(2):
                 k = 4 * slot + 2 * c + part
                 lanes = slice(c * tile, (c + 1) * tile)
-                first, second, weight = (
+                first, weight = (
                     decode(shadow_q[i, at, here, lanes], shadow_s[i, at, :, lanes])
-                    for i in range(3)
+                    for i in range(2)
                 )
+                root = shadow_q[2, at, here, lanes].astype(jnp.int32).astype(F32)
+                root = root * (ROOT_SPAN / LEVELS) + ROOT_MID
+                second = root * root
                 clipped = decode(q_in[0, mid, k, here, :], s_in[0, mid, k]) * factor
                 first = 0.9 * first + 0.1 * clipped
                 second = 0.95 * second + 0.05 * clipped * clipped
@@ -646,7 +701,12 @@
             at = slot * 2 + part - (blocks - SHADOW)
             if part == 0 and 4 * slot + 4 > RES:
                 late(slot)
-            step_rows(slot, part)
+            if slot + part == 0:
+                for r in range(half // slab):
+                    step_rows(0, 0, r, r + 1)
+                    spread_slab(r)
+            else:
+                step_rows(slot, part)
             if at >= 0:
 
                 @pl.when(jnp.logical_not(at_end))
@@ -655,7 +715,8 @@
 
             if slot == 0:
                 mine(part).start()
-                spread(piece(mp, part), mp, part)
+                if part:
+                    spread(piece(mp, part), mp, part)
             else:
                 to_head(slot, part).start()
 
@@ -782,8 +843,7 @@
             owned,
             jax.ShapeDtypeStruct((rows * dpn * heads, cols // heads), jnp.bfloat16),
         ),
-        in_specs=[pl.BlockSpec(memory_space=pltpu.SMEM)]
-        + [hbm] * 5,
+        in_specs=[pl.BlockSpec(memory_space=pltpu.SMEM)] + [hbm] * 5,
         out_specs=(hbm,) * 4,
         scratch_shapes=[
             pltpu.VMEM((line, 2 * tokens, rows), jnp.bfloat16),
@@ -804,7 +864,7 @@
             wide,
             pltpu.VMEM((2 * heads + SHADOW, rows // 2, 2 * tile), jnp.bfloat16),
             pltpu.VMEM((3, SHADOW, rows // 2, 2 * tile), jnp.int16),
-            pltpu.VMEM((3, SHADOW, 1, 2 * tile), F32),
+            pltpu.VMEM((2, SHADOW, 1, 2 * tile), F32),
             dma((line + heads,)),
             dma((2,)),
             dma((line + heads + 2,)),

time: 78.3 us -> 77.5 us (0.990)
  Pallas kernels: 76.9 us -> 76 us
    pallas_call x1, Pallas kernels: 73.8 us -> 73 us  [one_kernel(): pl.pallas_call(functools.partial(kernel, line, heads, clip_total), out_sh...]
where the time goes in v4:
time: 77.5 us; the launch traced here: 77.3 us
  Pallas kernels  76 us (98%)
  between operations  1.29 us (2%)
    pallas_call x1, Pallas kernels, one_kernel(): pl.pallas_call(functools.partial(kernel, line, heads, clip_total), out_sh...  73 us
    pallas_call x1, Pallas kernels, one_kernel(): pl.pallas_call(settle, out_shape=shapes, in_specs=[hbm] * 4, out_specs=(h...  3.05 us

profile of v4, /device:TPU:0, one launch (start us, length us, event | category | flops | bytes accessed | tf_op | source)
XLA Modules:
  0.0 77.3 jit_solution(6314458502967878512)
XLA Ops:
  1.3 73.0 %shard_map.93 = (f32[256,1024]{1,0:T(8,128)S(1)}, f32[256,1024]{1,0:T(8,128)S(1)}, f32[256,1024]{1,0:T(8,128)S(1)}, bf16[8192,256]{1,0:T(8,128)(2,1)S(1)}) custom-call(s32[1]{0:T(128)S(6)} %copy.10.step_ref, bf16[512,2048]{1,0:T(8,128)(2,1)} %act_ref.1, bf16[512,1024]{1,0:T(8,128)(2,1)} %vg_ref.1, f32[256,1024]{1,0:T(8,128)} %master_ref.1, ...), custom_call_target="tpu_custom_call" | custom-call | tf_op jit(solution)/shard_map/pallas_call | solution.py:838
  74.3 3.0 %shard_map.94 = (f32[256,1024]{1,0:T(8,128)}, f32[256,1024]{1,0:T(8,128)}, f32[256,1024]{1,0:T(8,128)}, bf16[8192,256]{1,0:T(8,128)(2,1)}) custom-call(f32[256,1024]{1,0:T(8,128)S(1)} %get-tuple-element.8.refs_0_, f32[256,1024]{1,0:T(8,128)S(1)} %get-tuple-element.9.refs_1_, f32[256,1024]{1,0:T(8,128)S(1)} %get-tuple-element.10.refs_2_, ...), custom_call_target="tpu_custom_call" | custom-call | tf_op jit(solution)/shard_map/pallas_call | solution.py:892

commit v5 on v4

--- a/solution.py
+++ b/solution.py
@@ -12,10 +12,10 @@
 LEVELS = 32760.0
 PIECES = (1, 1, 1, 4)
 RES = 5
-LAG = 5
+LAG = 4
 EARLY = 3
 SHADOW = 3
-LENT = (5, 7)
+LENT = (4, 7)
 ROOT_MID = (1.0 + math.sqrt(0.05)) / 2
 ROOT_SPAN = (1.0 - math.sqrt(0.05)) / 2
 MESH = pl.DeviceIdType.MESH
@@ -449,7 +449,9 @@
                 heard(0)
                 hello(1)
 
-        @pl.loop(2 * units - LAG, 2 * units - RES)
+        left = min(LAG, RES)
+
+        @pl.loop(2 * units - LAG, 2 * units - left)
         def _(j):
             with jax.named_scope("Mf"):
                 onward(j)
@@ -459,7 +461,10 @@
         @pl.loop(0, RES)
         def _(k):
             with jax.named_scope("Mr"):
-                onward(2 * units - RES + k)
+                @pl.when(k < left)
+                def _():
+                    onward(2 * units - left + k)
+
                 total = take(mid, k, 0, 2 * units + k)
                 acc[mid, *unit(k)] = total
                 add_squares(total)

time: 77.5 us -> 77 us (level)
  no operation moved by 1% of the time
where the time goes in v5:
time: 77 us; the launch traced here: 76.8 us
  Pallas kernels  75.5 us (98%)
  between operations  1.29 us (2%)
    pallas_call x1, Pallas kernels, one_kernel(): pl.pallas_call(functools.partial(kernel, line, heads, clip_total), out_sh...  72.5 us
    pallas_call x1, Pallas kernels, one_kernel(): pl.pallas_call(settle, out_shape=shapes, in_specs=[hbm] * 4, out_specs=(h...  3.05 us

profile of v5, /device:TPU:0, one launch (start us, length us, event | category | flops | bytes accessed | tf_op | source)
XLA Modules:
  0.0 76.8 jit_solution(9115159322433451366)
XLA Ops:
  1.3 72.5 %shard_map.93 = (f32[256,1024]{1,0:T(8,128)S(1)}, f32[256,1024]{1,0:T(8,128)S(1)}, f32[256,1024]{1,0:T(8,128)S(1)}, bf16[8192,256]{1,0:T(8,128)(2,1)S(1)}) custom-call(s32[1]{0:T(128)S(6)} %copy.10.step_ref, bf16[512,2048]{1,0:T(8,128)(2,1)} %act_ref.1, bf16[512,1024]{1,0:T(8,128)(2,1)} %vg_ref.1, f32[256,1024]{1,0:T(8,128)} %master_ref.1, ...), custom_call_target="tpu_custom_call" | custom-call | tf_op jit(solution)/shard_map/pallas_call | solution.py:843
  73.8 3.0 %shard_map.94 = (f32[256,1024]{1,0:T(8,128)}, f32[256,1024]{1,0:T(8,128)}, f32[256,1024]{1,0:T(8,128)}, bf16[8192,256]{1,0:T(8,128)(2,1)}) custom-call(f32[256,1024]{1,0:T(8,128)S(1)} %get-tuple-element.8.refs_0_, f32[256,1024]{1,0:T(8,128)S(1)} %get-tuple-element.9.refs_1_, f32[256,1024]{1,0:T(8,128)S(1)} %get-tuple-element.10.refs_2_, ...), custom_call_target="tpu_custom_call" | custom-call | tf_op jit(solution)/shard_map/pallas_call | solution.py:897
